TPU v7x, 128 devices: a whole 4x4x4 slice. The times are simulated.
128 devices in a mesh: grp: 4 (over z), slab: 32 (over x, y, core).
Axes of the slice: x: 4, y: 4, z: 4, core: 2. Of those that a mesh axis runs over, the one named last changes fastest.
Arguments:
- probes: float32 [64, 512, 8, 512], P(None, 'slab', None, 'grp'), may hold values from -6 to 6
- courant: float32 [512, 8, 512], P('slab', None, 'grp'), may hold values from 0.02 to 0.18
- rec_cell: int32 [8192], P(('grp', 'slab')), may hold values from 0 to 16383
- rec_owner: int32 [8192, 1], P(('grp', 'slab')), may hold values from 0 to 31; in each aligned block of 64 rows (0 to 63, 64 to 127, ...) at most 8 rows name the same one
- trace_weight: float32 [8192], P(('grp', 'slab')), may hold values from 1 to 10
Outputs:
- wavefield: float32 [64, 512, 8, 512], P(None, 'slab', None, 'grp')
- q_basis: float32 [32768, 256], P(('grp', 'slab'))
- r_factor: float32 [64, 64], replicated
Inputs may be any that keep to these rules, and one draw needn't show every extreme that they name: `rec_owner`: among the receivers of one device no owner is named by more than 8; in every draw some device names some owner exactly 8 times.
All inputs are finite; a program needn't handle non-finite values.
Results may differ from a plain program's by a relative error of at most 0.00016.
Values sent between devices are 32-bit elements; how exact they have to be, the bound alone decides.
A program may use at most 192 MiB of HBM per device.

v0:
```python
import math

import jax
import jax.numpy as jnp
from jax import lax
from jax.sharding import PartitionSpec as P

PROBES = 64
CX = 16
CY = 8
CZ = 128
STEPS = 4


stencil_weights = (-205.0 / 72.0, 8.0 / 5.0, -1.0 / 5.0, 8.0 / 315.0, -1.0 / 560.0)


def with_halo(block, sides, width):
    for axis, dim in sides:
        count = lax.axis_size(axis)
        forward = [(i, i + 1) for i in range(count - 1)]
        backward = [(target, source) for source, target in forward]
        low = lax.ppermute(
            lax.slice_in_dim(block, block.shape[dim] - width, None, axis=dim), axis, forward
        )
        high = lax.ppermute(lax.slice_in_dim(block, 0, width, axis=dim), axis, backward)
        block = jnp.concatenate([low, block, high], axis=dim)
    return block


def laplace(padded):
    size_x = padded.shape[1] - 8
    size_y = padded.shape[2] - 8
    size_z = padded.shape[3] - 8
    center = padded[:, 4 : 4 + size_x, 4 : 4 + size_y, 4 : 4 + size_z]
    total = 3.0 * stencil_weights[0] * center
    for offset in range(1, 5):
        beside_all = padded[:, 4 + offset : 4 + offset + size_x, 4 : 4 + size_y, 4 : 4 + size_z]
        beside_all = (
            beside_all + padded[:, 4 - offset : 4 - offset + size_x, 4 : 4 + size_y, 4 : 4 + size_z]
        )
        beside_all = (
            beside_all + padded[:, 4 : 4 + size_x, 4 + offset : 4 + offset + size_y, 4 : 4 + size_z]
        )
        beside_all = (
            beside_all + padded[:, 4 : 4 + size_x, 4 - offset : 4 - offset + size_y, 4 : 4 + size_z]
        )
        beside_all = (
            beside_all + padded[:, 4 : 4 + size_x, 4 : 4 + size_y, 4 + offset : 4 + offset + size_z]
        )
        beside_all = (
            beside_all + padded[:, 4 : 4 + size_x, 4 : 4 + size_y, 4 - offset : 4 - offset + size_z]
        )
        total = total + stencil_weights[offset] * beside_all
    return total


def pad_middle(field):
    return jnp.pad(field, ((0, 0), (0, 0), (4, 4), (0, 0)))


def per_device(probes, courant, rec_cell, rec_owner, trace_weight):
    n_slab = lax.axis_size("slab")
    n_group = lax.axis_size("grp")
    rec_count = rec_cell.shape[0]
    capacity = max(2, 4 * rec_count // n_slab)
    cells = CX * CY * CZ
    picker = (jnp.arange(cells, dtype=jnp.int32)[:, None] == rec_cell[None, :]).astype(jnp.float32)
    speed = courant[None]
    previous = probes
    current = probes
    samples = []
    for moment in range(STEPS):
        extended = with_halo(current, (("grp", 3), ("slab", 1)), 4)
        advanced = 2.0 * current - previous + speed * laplace(pad_middle(extended))
        previous = current
        current = advanced
        samples.append(
            jnp.dot(
                current.reshape(PROBES, cells),
                picker,
                preferred_element_type=jnp.float32,
                precision=lax.Precision.HIGHEST,
            )
        )
    traces = jnp.stack(samples)
    rows = jnp.transpose(traces, (2, 0, 1)) * trace_weight[:, None, None]
    rows = rows.reshape(rec_count, STEPS * PROBES)
    sketch = rows.reshape(rec_count * STEPS, PROBES)
    gram = jnp.dot(
        sketch.T, sketch, preferred_element_type=jnp.float32, precision=lax.Precision.HIGHEST
    )
    owners = rec_owner[:, 0]
    hits = (owners[:, None] == jnp.arange(n_slab, dtype=jnp.int32)[None, :]).astype(jnp.int32)
    before = jnp.cumsum(hits, axis=0) - hits
    slots = jnp.sum(before * hits, axis=1)
    target = owners * capacity + slots
    placer = (target[:, None] == jnp.arange(n_slab * capacity, dtype=jnp.int32)[None, :]).astype(
        jnp.float32
    )
    outgoing = jnp.dot(
        placer.T, rows, preferred_element_type=jnp.float32, precision=lax.Precision.HIGHEST
    )
    incoming = lax.all_to_all(
        outgoing.reshape(n_slab, capacity, STEPS * PROBES),
        "slab",
        split_axis=0,
        concat_axis=0,
        tiled=True,
    )
    incoming = incoming.reshape(n_slab * capacity, STEPS * PROBES)
    lower = jnp.linalg.cholesky(lax.psum(gram, ("grp", "slab")))
    row_count = rec_count * n_slab * n_group * STEPS
    r_factor = lower.T / math.sqrt(row_count)
    solved = jax.scipy.linalg.solve_triangular(
        lower, incoming.reshape(n_slab * capacity * STEPS, PROBES).T, lower=True
    )
    q_basis = (solved.T * math.sqrt(row_count)).reshape(n_slab * capacity, STEPS * PROBES)
    return (current, q_basis, r_factor)


def solution(mesh):
    return jax.shard_map(
        per_device,
        mesh=mesh,
        in_specs=(
            P(None, "slab", None, "grp"),
            P("slab", None, "grp"),
            P(("grp", "slab")),
            P(("grp", "slab"), None),
            P(("grp", "slab")),
        ),
        out_specs=(P(None, "slab", None, "grp"), P(("grp", "slab"), None), P()),
        check_vma=False,
    )
```

profile of v0, /device:TPU:1, one launch (start us, length us, event | category | flops | bytes accessed | tf_op | source)
XLA Modules:
  0.0 824.6 jit_solution(537160318076101467)
XLA Ops:
  0.6 8.2 fusion.137
  17.5 5.0 collective-permute-start
  22.9 4.6 copy.90
  27.5 4.5 copy.89
  32.0 4.7 pad_maximum_fusion.21
  36.7 4.8 collective-permute-start.3
  43.6 20.9 %collective-permute-done.3 = f32[64,4,8,136]{3,2,1,0:T(8,128)S(1)} collective-permute-done((f32[64,4,8,136]{3,2,1,0:T(8,128)S(1)}, f32[64,4,8,136]{3,2,1,0:T(8,128)S(1)}, u32[]{:S(2)}, u32[]{:S(2)}) %collective-permute-start.3) | collective-permute-done | bytes 1114144 | tf_op jit(solution)/shard_map/ppermute | solution.py:23
  64.5 4.4 collective-permute-done.2
  68.9 11.0 %pad_maximum_fusion = (f32[64,20,8,136]{3,2,1,0:T(8,128)}, f32[64,20,8,136]{3,2,1,0:T(8,128)}) fusion(f32[64,4,8,136]{3,2,1,0:T(8,128)S(1)} %collective-permute-done.2, f32[64,16,8,4]{3,2,1,0:T(8,128)S(1)} %copy-done.8, f32[64,16,8,128]{3,2,1,0:T(8,128)S(1)} %copy-done.5, f32[64,16,8,4]{3,2,1,0:T(8,128)S(1)} %copy-done.11, ...), kind=kLoop, calls=%fused_computation.67 | loop fusion | flops 8355840 | bytes 17825792 | tf_op jit(solution)/shard_map/concatenate | solution.py:27
  79.9 12.4 %select_maximum_fusion.12 = f32[64,24,16,136]{3,2,1,0:T(8,128)} fusion(f32[64,4,8,136]{3,2,1,0:T(8,128)S(1)} %collective-permute-done.2, f32[64,4,8,136]{3,2,1,0:T(8,128)S(1)} %collective-permute-done.3, f32[64,16,8,4]{3,2,1,0:T(8,128)S(1)} %copy-done.8, f32[64,16,8,128]{3,2,1,0:T(8,128)S(1)} %copy-done.5, f32[64,16,8,4]{3,2,1,0:T(8,128)S(1)} %copy-done.11), kind=kLoop, calls=%fused_computation.14 | loop fusion | flops 40108032 | bytes 20054016 | tf_op jit(solution)/shard_map/concatenate | solution.py:27
  92.3 88.4 %fusion.1 = f32[64,16,8,128]{3,2,1,0:T(8,128)} fusion(f32[64,16,8,128]{3,2,1,0:T(8,128)} %param.5, f32[64,16,8,4]{3,2,1,0:T(8,128)} %copy.89, f32[64,16,8,4]{3,2,1,0:T(8,128)} %copy.90, f32[64,24,16,136]{3,2,1,0:T(8,128)} %select_maximum_fusion.12, f32[64,20,8,136]{3,2,1,0:T(8,128)} %get-tuple-element.34, f32[64,20,8,136]{3,2,1,0:T(8,128)} %get-tuple-element.33, ...), kind=kLoop, calls=%fused_computation.76 | loop fusion | flops 42991616 | bytes 75825152 | tf_op jit(solution)/shard_map/add | solution.py:75
  180.7 8.2 fusion.136
  197.6 4.7 collective-permute-start.4
  202.4 4.6 copy.96
  207.0 4.5 copy.95
  211.5 4.7 pad_maximum_fusion.18
  221.9 20.6 %collective-permute-done.7 = f32[64,4,8,136]{3,2,1,0:T(8,128)S(1)} collective-permute-done((f32[64,4,8,136]{3,2,1,0:T(8,128)S(1)}, f32[64,4,8,136]{3,2,1,0:T(8,128)S(1)}, u32[]{:S(2)}, u32[]{:S(2)}) %collective-permute-start.7) | collective-permute-done | bytes 1114144 | tf_op jit(solution)/shard_map/ppermute | solution.py:23
  242.5 4.4 collective-permute-done.6
  246.9 11.0 %pad_maximum_fusion.1 = (f32[64,20,8,136]{3,2,1,0:T(8,128)}, f32[64,20,8,136]{3,2,1,0:T(8,128)}) fusion(f32[64,4,8,136]{3,2,1,0:T(8,128)S(1)} %collective-permute-done.6, f32[64,16,8,4]{3,2,1,0:T(8,128)S(1)} %copy-done.9, f32[64,16,8,128]{3,2,1,0:T(8,128)S(1)} %copy-done, f32[64,16,8,4]{3,2,1,0:T(8,128)S(1)} %copy-done.12, ...), kind=kLoop, calls=%fused_computation.69 | loop fusion | flops 8355840 | bytes 17825792 | tf_op jit(solution)/shard_map/concatenate | solution.py:27
  257.9 12.4 %select_maximum_fusion.8 = f32[64,24,16,136]{3,2,1,0:T(8,128)} fusion(f32[64,4,8,136]{3,2,1,0:T(8,128)S(1)} %collective-permute-done.6, f32[64,4,8,136]{3,2,1,0:T(8,128)S(1)} %collective-permute-done.7, f32[64,16,8,4]{3,2,1,0:T(8,128)S(1)} %copy-done.9, f32[64,16,8,128]{3,2,1,0:T(8,128)S(1)} %copy-done, f32[64,16,8,4]{3,2,1,0:T(8,128)S(1)} %copy-done.12), kind=kLoop, calls=%fused_computation.10 | loop fusion | flops 40108032 | bytes 20054016 | tf_op jit(solution)/shard_map/concatenate | solution.py:27
  270.4 88.6 %fusion.50 = f32[64,16,8,128]{3,2,1,0:T(8,128)} fusion(f32[64,16,8,4]{3,2,1,0:T(8,128)} %copy.95, f32[64,16,8,128]{3,2,1,0:T(8,128)} %fusion.1, f32[64,16,8,4]{3,2,1,0:T(8,128)} %copy.96, f32[64,24,16,136]{3,2,1,0:T(8,128)} %select_maximum_fusion.8, f32[64,20,8,136]{3,2,1,0:T(8,128)} %get-tuple-element.30, f32[64,20,8,136]{3,2,1,0:T(8,128)} %get-tuple-element.29, ...), kind=kLoop, calls=%fused_computation.125 | loop fusion | flops 42991616 | bytes 80019456 | tf_op jit(solution)/shard_map/add | solution.py:75
  359.0 8.2 fusion.135
  375.8 4.9 collective-permute-start.8
  380.8 4.6 copy.102
  385.4 4.5 copy.101
  389.8 4.7 pad_maximum_fusion.15
  399.3 21.0 %collective-permute-done.11 = f32[64,4,8,136]{3,2,1,0:T(8,128)S(1)} collective-permute-done((f32[64,4,8,136]{3,2,1,0:T(8,128)S(1)}, f32[64,4,8,136]{3,2,1,0:T(8,128)S(1)}, u32[]{:S(2)}, u32[]{:S(2)}) %collective-permute-start.11) | collective-permute-done | bytes 1114144 | tf_op jit(solution)/shard_map/ppermute | solution.py:23
  424.8 11.0 %pad_maximum_fusion.2 = (f32[64,20,8,136]{3,2,1,0:T(8,128)}, f32[64,20,8,136]{3,2,1,0:T(8,128)}) fusion(f32[64,4,8,136]{3,2,1,0:T(8,128)S(1)} %collective-permute-done.10, f32[64,16,8,4]{3,2,1,0:T(8,128)S(1)} %copy-done.10, f32[64,16,8,128]{3,2,1,0:T(8,128)S(1)} %copy-done.2, f32[64,16,8,4]{3,2,1,0:T(8,128)S(1)} %copy-done.13, ...), kind=kLoop, calls=%fused_computation.71 | loop fusion | flops 8355840 | bytes 17825792 | tf_op jit(solution)/shard_map/concatenate | solution.py:27
  435.8 12.4 %select_maximum_fusion.4 = f32[64,24,16,136]{3,2,1,0:T(8,128)} fusion(f32[64,4,8,136]{3,2,1,0:T(8,128)S(1)} %collective-permute-done.10, f32[64,4,8,136]{3,2,1,0:T(8,128)S(1)} %collective-permute-done.11, f32[64,16,8,4]{3,2,1,0:T(8,128)S(1)} %copy-done.10, f32[64,16,8,128]{3,2,1,0:T(8,128)S(1)} %copy-done.2, f32[64,16,8,4]{3,2,1,0:T(8,128)S(1)} %copy-done.13), kind=kLoop, calls=%fused_computation.6 | loop fusion | flops 40108032 | bytes 20054016 | tf_op jit(solution)/shard_map/concatenate | solution.py:27
  448.2 89.1 %fusion.29 = f32[64,16,8,128]{3,2,1,0:T(8,128)} fusion(f32[64,16,8,4]{3,2,1,0:T(8,128)} %copy.101, f32[64,16,8,128]{3,2,1,0:T(8,128)} %fusion.50, f32[64,16,8,4]{3,2,1,0:T(8,128)} %copy.102, f32[64,24,16,136]{3,2,1,0:T(8,128)} %select_maximum_fusion.4, f32[64,20,8,136]{3,2,1,0:T(8,128)} %get-tuple-element.26, f32[64,20,8,136]{3,2,1,0:T(8,128)} %get-tuple-element.25, ...), kind=kLoop, calls=%fused_computation.104 | loop fusion | flops 42991616 | bytes 80019456 | tf_op jit(solution)/shard_map/add | solution.py:75
  537.3 8.2 fusion.134
  559.0 5.5 collective-permute-done.13
  564.5 4.6 copy.108
  569.0 4.6 copy.107
  573.6 4.7 pad_maximum_fusion.12
  584.0 4.7 fusion.113
  588.7 4.7 fusion.116
  593.4 4.8 fusion.119
  598.2 6.8 collective-permute-done.15
  605.0 4.7 collective-permute-done.14
  609.7 11.0 %pad_maximum_fusion.3 = (f32[64,20,8,136]{3,2,1,0:T(8,128)}, f32[64,20,8,136]{3,2,1,0:T(8,128)}) fusion(f32[64,4,8,136]{3,2,1,0:T(8,128)S(1)} %collective-permute-done.14, f32[64,16,8,4]{3,2,1,0:T(8,128)S(1)} %copy-done.6, f32[64,16,8,128]{3,2,1,0:T(8,128)S(1)} %copy-done.4, f32[64,16,8,4]{3,2,1,0:T(8,128)S(1)} %copy-done.7, ...), kind=kLoop, calls=%fused_computation.73 | loop fusion | flops 8355840 | bytes 17825792 | tf_op jit(solution)/shard_map/concatenate | solution.py:27
  620.7 12.4 %select_maximum_fusion = f32[64,24,16,136]{3,2,1,0:T(8,128)} fusion(f32[64,4,8,136]{3,2,1,0:T(8,128)S(1)} %collective-permute-done.14, f32[64,4,8,136]{3,2,1,0:T(8,128)S(1)} %collective-permute-done.15, f32[64,16,8,4]{3,2,1,0:T(8,128)S(1)} %copy-done.6, f32[64,16,8,128]{3,2,1,0:T(8,128)S(1)} %copy-done.4, f32[64,16,8,4]{3,2,1,0:T(8,128)S(1)} %copy-done.7), kind=kLoop, calls=%fused_computation.2 | loop fusion | flops 40108032 | bytes 20054016 | tf_op jit(solution)/shard_map/concatenate | solution.py:27
  633.2 89.8 %fusion.8 = f32[64,16,8,128]{3,2,1,0:T(8,128)} fusion(f32[64,16,8,4]{3,2,1,0:T(8,128)} %copy.107, f32[64,16,8,128]{3,2,1,0:T(8,128)} %fusion.29, f32[64,16,8,4]{3,2,1,0:T(8,128)} %copy.108, f32[64,24,16,136]{3,2,1,0:T(8,128)} %select_maximum_fusion, f32[64,20,8,136]{3,2,1,0:T(8,128)} %get-tuple-element.22, f32[64,20,8,136]{3,2,1,0:T(8,128)} %get-tuple-element.21, ...), kind=kLoop, calls=%fused_computation.83 | loop fusion | flops 42991616 | bytes 80019456 | tf_op jit(solution)/shard_map/add | solution.py:75
  723.0 6.7 fusion.122
  730.0 70.9 %psum.7 = f32[64,64]{0,1:T(8,128)S(1)} all-reduce(f32[64,64]{0,1:T(8,128)S(1)} %convolution_bitcast_fusion), channel_id=1, replica_groups=mesh['grp'=4,'slab'=32] {'grp','slab'}, use_global_device_ids=true, to_apply=%region_2.3 | all-reduce | flops 4096 | bytes 32768 | tf_op jit(solution)/shard_map/psum | solution.py:112
  801.0 5.8 cholesky.16
  807.9 5.5 all-to-all-start
  815.4 4.9 custom-call.7
  (83 shorter events, 70.2 us)
Async XLA Ops:
  12.5 10.4 %collective-permute-start.1 = (f32[64,16,8,4]{0,2,3,1:T(8,128)S(1)}, f32[64,16,8,4]{0,2,3,1:T(8,128)S(1)}, u32[]{:S(2)}, u32[]{:S(2)}) collective-permute-start(f32[64,16,8,4]{0,2,3,1:T(8,128)S(1)} %copy.123), channel_id=1, source_target_pairs={{32,0},{64,32},{96,64},{33,1},{65,33},{97,65},{34,2},{66,34},{98,6... | collective-permute-start | bytes 393224 | tf_op jit(solution)/shard_map/ppermute | solution.py:26
  17.5 10.0 %collective-permute-start = (f32[64,16,8,4]{0,2,3,1:T(8,128)S(1)}, f32[64,16,8,4]{0,2,3,1:T(8,128)S(1)}, u32[]{:S(2)}, u32[]{:S(2)}) collective-permute-start(f32[64,16,8,4]{0,2,3,1:T(8,128)S(1)} %copy.122), channel_id=1, source_target_pairs={{0,32},{32,64},{64,96},{1,33},{33,65},{65,97},{2,34},{34,66},{66,9... | collective-permute-start | bytes 393224 | tf_op jit(solution)/shard_map/ppermute | solution.py:23
  32.0 36.9 %copy-start.5 = (f32[64,16,8,128]{3,2,1,0:T(8,128)S(1)}, f32[64,16,8,128]{3,2,1,0:T(8,128)}, u32[]{:S(2)}) copy-start(f32[64,16,8,128]{3,2,1,0:T(8,128)} %param.5) | copy-start | bytes 12582916
  32.0 36.9 %copy-start.8 = (f32[64,16,8,4]{3,2,1,0:T(8,128)S(1)}, f32[64,16,8,4]{3,2,1,0:T(8,128)}, u32[]{:S(2)}) copy-start(f32[64,16,8,4]{3,2,1,0:T(8,128)} %copy.90) | copy-start | bytes 393220
  32.0 36.9 %copy-start.11 = (f32[64,16,8,4]{3,2,1,0:T(8,128)S(1)}, f32[64,16,8,4]{3,2,1,0:T(8,128)}, u32[]{:S(2)}) copy-start(f32[64,16,8,4]{3,2,1,0:T(8,128)} %copy.89) | copy-start | bytes 393220
  36.7 27.8 %collective-permute-start.3 = (f32[64,4,8,136]{3,2,1,0:T(8,128)S(1)}, f32[64,4,8,136]{3,2,1,0:T(8,128)S(1)}, u32[]{:S(2)}, u32[]{:S(2)}) collective-permute-start(f32[64,4,8,136]{3,2,1,0:T(8,128)S(1)} %get-tuple-element.35), channel_id=1, source_target_pairs={{0,1},{1,2},{2,3},{3,4},{4,5},{5,6},{6,7},{7,8},{8,9},{9,10},{10,1... | collective-permute-start | bytes 3342344 | tf_op jit(solution)/shard_map/ppermute | solution.py:23
  41.5 27.4 %collective-permute-start.2 = (f32[64,4,8,136]{3,2,1,0:T(8,128)S(1)}, f32[64,4,8,136]{3,2,1,0:T(8,128)S(1)}, u32[]{:S(2)}, u32[]{:S(2)}) collective-permute-start(f32[64,4,8,136]{3,2,1,0:T(8,128)S(1)} %get-tuple-element.36), channel_id=1, source_target_pairs={{1,0},{2,1},{3,2},{4,3},{5,4},{6,5},{7,6},{8,7},{9,8},{10,9},{11,1... | collective-permute-start | bytes 3342344 | tf_op jit(solution)/shard_map/ppermute | solution.py:26
  79.9 12.4 %copy-start.14 = (f32[16,8,128]{2,1,0:T(8,128)S(1)}, f32[16,8,128]{2,1,0:T(8,128)}, u32[]{:S(2)}) copy-start(f32[16,8,128]{2,1,0:T(8,128)} %param.6) | copy-start | bytes 196612
  192.6 9.8 %collective-permute-start.5 = (f32[64,16,8,4]{0,2,3,1:T(8,128)S(1)}, f32[64,16,8,4]{0,2,3,1:T(8,128)S(1)}, u32[]{:S(2)}, u32[]{:S(2)}) collective-permute-start(f32[64,16,8,4]{0,2,3,1:T(8,128)S(1)} %copy.94), channel_id=1, source_target_pairs={{32,0},{64,32},{96,64},{33,1},{65,33},{97,65},{34,2},{66,34},{98,6... | collective-permute-start | bytes 393224 | tf_op jit(solution)/shard_map/ppermute | solution.py:26
  197.6 9.4 %collective-permute-start.4 = (f32[64,16,8,4]{0,2,3,1:T(8,128)S(1)}, f32[64,16,8,4]{0,2,3,1:T(8,128)S(1)}, u32[]{:S(2)}, u32[]{:S(2)}) collective-permute-start(f32[64,16,8,4]{0,2,3,1:T(8,128)S(1)} %copy.93), channel_id=1, source_target_pairs={{0,32},{32,64},{64,96},{1,33},{33,65},{65,97},{2,34},{34,66},{66,9... | collective-permute-start | bytes 393224 | tf_op jit(solution)/shard_map/ppermute | solution.py:23
  211.5 35.5 %copy-start = (f32[64,16,8,128]{3,2,1,0:T(8,128)S(1)}, f32[64,16,8,128]{3,2,1,0:T(8,128)}, u32[]{:S(2)}) copy-start(f32[64,16,8,128]{3,2,1,0:T(8,128)} %fusion.1) | copy-start | bytes 12582916
  211.5 35.5 %copy-start.9 = (f32[64,16,8,4]{3,2,1,0:T(8,128)S(1)}, f32[64,16,8,4]{3,2,1,0:T(8,128)}, u32[]{:S(2)}) copy-start(f32[64,16,8,4]{3,2,1,0:T(8,128)} %copy.96) | copy-start | bytes 393220
  211.5 35.5 %copy-start.12 = (f32[64,16,8,4]{3,2,1,0:T(8,128)S(1)}, f32[64,16,8,4]{3,2,1,0:T(8,128)}, u32[]{:S(2)}) copy-start(f32[64,16,8,4]{3,2,1,0:T(8,128)} %copy.95) | copy-start | bytes 393220
  216.1 26.4 %collective-permute-start.7 = (f32[64,4,8,136]{3,2,1,0:T(8,128)S(1)}, f32[64,4,8,136]{3,2,1,0:T(8,128)S(1)}, u32[]{:S(2)}, u32[]{:S(2)}) collective-permute-start(f32[64,4,8,136]{3,2,1,0:T(8,128)S(1)} %get-tuple-element.31), channel_id=1, source_target_pairs={{0,1},{1,2},{2,3},{3,4},{4,5},{5,6},{6,7},{7,8},{8,9},{9,10},{10,1... | collective-permute-start | bytes 3342344 | tf_op jit(solution)/shard_map/ppermute | solution.py:23
  219.6 27.4 %collective-permute-start.6 = (f32[64,4,8,136]{3,2,1,0:T(8,128)S(1)}, f32[64,4,8,136]{3,2,1,0:T(8,128)S(1)}, u32[]{:S(2)}, u32[]{:S(2)}) collective-permute-start(f32[64,4,8,136]{3,2,1,0:T(8,128)S(1)} %get-tuple-element.32), channel_id=1, source_target_pairs={{1,0},{2,1},{3,2},{4,3},{5,4},{6,5},{7,6},{8,7},{9,8},{10,9},{11,1... | collective-permute-start | bytes 3342344 | tf_op jit(solution)/shard_map/ppermute | solution.py:26
  370.8 9.9 %collective-permute-start.9 = (f32[64,16,8,4]{0,2,3,1:T(8,128)S(1)}, f32[64,16,8,4]{0,2,3,1:T(8,128)S(1)}, u32[]{:S(2)}, u32[]{:S(2)}) collective-permute-start(f32[64,16,8,4]{0,2,3,1:T(8,128)S(1)} %copy.100), channel_id=1, source_target_pairs={{32,0},{64,32},{96,64},{33,1},{65,33},{97,65},{34,2},{66,34},{98,6... | collective-permute-start | bytes 393224 | tf_op jit(solution)/shard_map/ppermute | solution.py:26
  375.8 9.5 %collective-permute-start.8 = (f32[64,16,8,4]{0,2,3,1:T(8,128)S(1)}, f32[64,16,8,4]{0,2,3,1:T(8,128)S(1)}, u32[]{:S(2)}, u32[]{:S(2)}) collective-permute-start(f32[64,16,8,4]{0,2,3,1:T(8,128)S(1)} %copy.99), channel_id=1, source_target_pairs={{0,32},{32,64},{64,96},{1,33},{33,65},{65,97},{2,34},{34,66},{66,9... | collective-permute-start | bytes 393224 | tf_op jit(solution)/shard_map/ppermute | solution.py:23
  389.8 34.9 %copy-start.2 = (f32[64,16,8,128]{3,2,1,0:T(8,128)S(1)}, f32[64,16,8,128]{3,2,1,0:T(8,128)}, u32[]{:S(2)}) copy-start(f32[64,16,8,128]{3,2,1,0:T(8,128)} %fusion.50) | copy-start | bytes 12582916
  389.8 34.9 %copy-start.10 = (f32[64,16,8,4]{3,2,1,0:T(8,128)S(1)}, f32[64,16,8,4]{3,2,1,0:T(8,128)}, u32[]{:S(2)}) copy-start(f32[64,16,8,4]{3,2,1,0:T(8,128)} %copy.102) | copy-start | bytes 393220
  389.8 34.9 %copy-start.13 = (f32[64,16,8,4]{3,2,1,0:T(8,128)S(1)}, f32[64,16,8,4]{3,2,1,0:T(8,128)}, u32[]{:S(2)}) copy-start(f32[64,16,8,4]{3,2,1,0:T(8,128)} %copy.101) | copy-start | bytes 393220
  394.5 25.9 %collective-permute-start.11 = (f32[64,4,8,136]{3,2,1,0:T(8,128)S(1)}, f32[64,4,8,136]{3,2,1,0:T(8,128)S(1)}, u32[]{:S(2)}, u32[]{:S(2)}) collective-permute-start(f32[64,4,8,136]{3,2,1,0:T(8,128)S(1)} %get-tuple-element.27), channel_id=1, source_target_pairs={{0,1},{1,2},{2,3},{3,4},{4,5},{5,6},{6,7},{7,8},{8,9},{9,10},{10,1... | collective-permute-start | bytes 3342344 | tf_op jit(solution)/shard_map/ppermute | solution.py:23
  397.4 27.4 %collective-permute-start.10 = (f32[64,4,8,136]{3,2,1,0:T(8,128)S(1)}, f32[64,4,8,136]{3,2,1,0:T(8,128)S(1)}, u32[]{:S(2)}, u32[]{:S(2)}) collective-permute-start(f32[64,4,8,136]{3,2,1,0:T(8,128)S(1)} %get-tuple-element.28), channel_id=1, source_target_pairs={{1,0},{2,1},{3,2},{4,3},{5,4},{6,5},{7,6},{8,7},{9,8},{10,9},{11,1... | collective-permute-start | bytes 3342344 | tf_op jit(solution)/shard_map/ppermute | solution.py:26
  545.4 13.2 %copy-start.16 = (s32[64,1]{0,1:T(1,128)S(1)}, s32[64,1]{0,1:T(1,128)}, u32[]{:S(2)}) copy-start(s32[64,1]{0,1:T(1,128)} %param.8) | copy-start | bytes 772
  552.8 16.2 %collective-permute-start.12 = (f32[64,16,8,4]{0,2,3,1:T(8,128)S(1)}, f32[64,16,8,4]{0,2,3,1:T(8,128)S(1)}, u32[]{:S(2)}, u32[]{:S(2)}) collective-permute-start(f32[64,16,8,4]{0,2,3,1:T(8,128)S(1)} %copy.105), channel_id=1, source_target_pairs={{0,32},{32,64},{64,96},{1,33},{33,65},{65,97},{2,34},{34,66},{66,9... | collective-permute-start | bytes 393224 | tf_op jit(solution)/shard_map/ppermute | solution.py:23
  557.0 7.5 collective-permute-start.13
  573.6 10.4 %copy-start.1 = (f32[64,16,8,128]{3,2,1,0:T(8,128)S(1)}, f32[64,16,8,128]{3,2,1,0:T(8,128)}, u32[]{:S(2)}) copy-start(f32[64,16,8,128]{3,2,1,0:T(8,128)} %fusion.1) | copy-start | bytes 12582916
  573.6 10.4 %copy-start.15 = (s32[64]{0:T(128)S(1)}, s32[64]{0:T(128)}, u32[]{:S(2)}) copy-start(s32[64]{0:T(128)} %param.7) | copy-start | bytes 772
  573.6 36.1 %copy-start.7 = (f32[64,16,8,4]{3,2,1,0:T(8,128)S(1)}, f32[64,16,8,4]{3,2,1,0:T(8,128)}, u32[]{:S(2)}) copy-start(f32[64,16,8,4]{3,2,1,0:T(8,128)} %copy.107) | copy-start | bytes 393220
  578.3 10.4 %copy-start.3 = (f32[64,16,8,128]{3,2,1,0:T(8,128)S(1)}, f32[64,16,8,128]{3,2,1,0:T(8,128)}, u32[]{:S(2)}) copy-start(f32[64,16,8,128]{3,2,1,0:T(8,128)} %fusion.50) | copy-start | bytes 12582916
  578.3 26.7 %collective-permute-start.15 = (f32[64,4,8,136]{3,2,1,0:T(8,128)S(1)}, f32[64,4,8,136]{3,2,1,0:T(8,128)S(1)}, u32[]{:S(2)}, u32[]{:S(2)}) collective-permute-start(f32[64,4,8,136]{3,2,1,0:T(8,128)S(1)} %get-tuple-element.23), channel_id=1, source_target_pairs={{0,1},{1,2},{2,3},{3,4},{4,5},{5,6},{6,7},{7,8},{8,9},{9,10},{10,1... | collective-permute-start | bytes 3342344 | tf_op jit(solution)/shard_map/ppermute | solution.py:23
  582.0 27.7 %collective-permute-start.14 = (f32[64,4,8,136]{3,2,1,0:T(8,128)S(1)}, f32[64,4,8,136]{3,2,1,0:T(8,128)S(1)}, u32[]{:S(2)}, u32[]{:S(2)}) collective-permute-start(f32[64,4,8,136]{3,2,1,0:T(8,128)S(1)} %get-tuple-element.24), channel_id=1, source_target_pairs={{1,0},{2,1},{3,2},{4,3},{5,4},{6,5},{7,6},{8,7},{9,8},{10,9},{11,1... | collective-permute-start | bytes 3342344 | tf_op jit(solution)/shard_map/ppermute | solution.py:26
  584.0 9.4 %copy-start.4 = (f32[64,16,8,128]{3,2,1,0:T(8,128)S(1)}, f32[64,16,8,128]{3,2,1,0:T(8,128)}, u32[]{:S(2)}) copy-start(f32[64,16,8,128]{3,2,1,0:T(8,128)} %fusion.29) | copy-start | bytes 12582916
  588.7 21.0 %copy-start.6 = (f32[64,16,8,4]{3,2,1,0:T(8,128)S(1)}, f32[64,16,8,4]{3,2,1,0:T(8,128)}, u32[]{:S(2)}) copy-start(f32[64,16,8,4]{3,2,1,0:T(8,128)} %copy.108) | copy-start | bytes 393220
  723.0 6.7 copy-start.17
  807.9 14.5 %all-to-all-start = ((f32[32,8,256]{2,1,0:T(8,128)}), f32[32,8,256]{2,1,0:T(8,128)S(1)}, u32[]{:S(2)}, u32[]{:S(2)}) async-start(f32[32,8,256]{2,1,0:T(8,128)} %fusion.126), calls=%async_computation | async-start | bytes 524288 | tf_op jit(solution)/shard_map/all_to_all | solution.py:104
where the time goes:
time: 832 us; the launch traced here: 825 us
  other arithmetic  481 us (58%)
  local copies, waits for them, and re-layouts  101 us (12%)
  waiting for transfers between devices  95.1 us (11%)
  blocking collectives  70.9 us (9%)
  starting transfers between devices  52.9 us (6%)
  matrix products  22.8 us (3%)
    add x4, other arithmetic, per_device(): advanced = 2.0 * current - previous + speed * laplace(pad_middle(extended))  356 us
    concatenate x12, other arithmetic, with_halo(): block = jnp.concatenate([low, block, high], axis=dim)  112 us
    psum x1, blocking collectives, per_device(): lower = jnp.linalg.cholesky(lax.psum(gram, ('grp', 'slab')))  70.9 us
    ppermute x8, waiting for transfers between devices, with_halo(): lax.ppermute(lax.slice_in_dim(block, block.shape[dim] - width, None, axis...  69.3 us
    slice x7, local copies, waits for them, and re-layouts, with_halo(): lax.slice_in_dim(block, 0, width, axis=dim)  43.7 us
    ppermute x8, starting transfers between devices, with_halo(): lax.ppermute(lax.slice_in_dim(block, block.shape[dim] - width, None, axis...  33.6 us
    ppermute x8, waiting for transfers between devices, with_halo(): lax.ppermute(lax.slice_in_dim(block, 0, width, axis=dim), axis, backward)  23.7 us
    dot_general x4, matrix products, per_device(): jnp.dot(current.reshape(PROBES, cells), picker, preferred_element_type=jn...  20.8 us
  transfers between devices with their start and end apart: 17, of which 11 were waited for; matrix products, arithmetic and copies ran while one was open for 6% of the time, Pallas kernels for 0%

commit v1 on v0

v1 whole, which is shorter than its diff:
```python
import functools
import math

import jax
import jax.numpy as jnp
from jax import lax
from jax.experimental import pallas as pl
from jax.experimental.pallas import tpu as pltpu
from jax.sharding import PartitionSpec as P

PROBES = 64
CX = 16
CY = 8
CZ = 128
STEPS = 4
CHUNK = 8
CHUNKS = PROBES // CHUNK
GROUP = 4
WIDTH = 4
CAP = 8
MESH = pl.DeviceIdType.MESH
EXACT = lax.Precision.HIGHEST

A0 = -205.0 / 72.0
A = (0.0, 8.0 / 5.0, -1.0 / 5.0, 8.0 / 315.0, -1.0 / 560.0)


def dot_nt(a, b):
    return lax.dot_general(
        a, b, (((1,), (1,)), ((), ())), precision=EXACT, preferred_element_type=jnp.float32
    )


def kernel(
    n_grp,
    n_slab,
    probes,
    courant,
    cell,
    owner,
    weight,
    wave_out,
    q_out,
    r_out,
    stage,
    first_halo,
    field,
    latest,
    speed,
    z_own,
    z_halo,
    z_fix,
    z_map,
    traces,
    outgoing,
    incoming,
    sum_a,
    sum_b,
    sum_c,
    load_sem,
    store_sem,
    x_send,
    x_recv,
    z_send,
    z_recv,
    a2a_send,
    a2a_recv,
    own_sem,
    sum_send,
    sum_recv,
):
    s = lax.axis_index("slab")
    g = lax.axis_index("grp")
    has = ((s > 0, s < n_slab - 1), (g > 0, g < n_grp - 1))

    def load(c):
        return pltpu.make_async_copy(
            probes.at[pl.ds(c * CHUNK, CHUNK)], stage.at[c], load_sem.at[c]
        )

    for c in range(CHUNKS):
        load(c).start()

    barrier = pltpu.get_barrier_semaphore()

    @pl.loop(1, n_slab)
    def _(k):
        pl.semaphore_signal(
            barrier, inc=1, device_id={"slab": lax.rem(s + k, n_slab)}, device_id_type=MESH
        )

    @pl.loop(1, n_grp)
    def _(k):
        pl.semaphore_signal(
            barrier, inc=1, device_id={"grp": lax.rem(g + k, n_grp)}, device_id_type=MESH
        )

    lane = lax.broadcasted_iota(jnp.int32, (8, 128), 1)
    edge = (lane < WIDTH) | (lane >= CZ - WIDTH)
    lane_slot = lane // 8
    low_half = (lane % 8) < WIDTH

    row_i = lax.broadcasted_iota(jnp.int32, (128, 128), 0)
    col_i = lax.broadcasted_iota(jnp.int32, (128, 128), 1)
    gap = jnp.abs(row_i - col_i)
    crossing = (row_i // 8 == col_i // 8) & ((row_i % 8 < WIDTH) != (col_i % 8 < WIDTH))
    table = jnp.zeros((128, 128), jnp.float32)
    for k in range(1, 5):
        table = jnp.where(gap == k, A[k], table)
    z_map[...] = jnp.where(crossing, table, 0.0)

    @pl.loop(0, CX)
    def _(x):
        for y in range(CY):
            speed[x, y] = jnp.broadcast_to(courant[x, pl.ds(y, 1), :], (8, 128))

    blank = jnp.zeros((WIDTH, CY, 8, 128), jnp.float32)
    for side in range(2):

        @pl.when(jnp.logical_not(has[0][side]))
        def _(side=side):
            @pl.loop(0, STEPS)
            def _(t):
                @pl.loop(0, CHUNKS)
                def _(c):
                    field[t, c, pl.ds(side * (CX + WIDTH), WIDTH)] = blank

        @pl.when(jnp.logical_not(has[1][side]))
        def _(side=side):
            @pl.loop(0, STEPS)
            def _(t):
                @pl.loop(0, CHUNKS)
                def _(c):
                    z_halo[side, t, c] = jnp.zeros((8, 8, 128), jnp.float32)

    def x_first(c, way):
        return pltpu.make_async_remote_copy(
            src_ref=probes.at[pl.ds(c * CHUNK, CHUNK), pl.ds((1 - way) * (CX - WIDTH) * CY, WIDTH * CY)],
            dst_ref=first_halo.at[way, c],
            send_sem=x_send.at[way, c],
            recv_sem=x_recv.at[way, 0, c],
            device_id={"slab": s + 1 - 2 * way},
            device_id_type=MESH,
        )

    def x_copy(t, c, way):
        return pltpu.make_async_remote_copy(
            src_ref=field.at[t, c, pl.ds(WIDTH + (1 - way) * (CX - WIDTH), WIDTH)],
            dst_ref=field.at[t, c, pl.ds(way * (CX + WIDTH), WIDTH)],
            send_sem=x_send.at[way, c],
            recv_sem=x_recv.at[way, t, c],
            device_id={"slab": s + 1 - 2 * way},
            device_id_type=MESH,
        )

    def z_copy(t, c, way):
        return pltpu.make_async_remote_copy(
            src_ref=z_own.at[t, c],
            dst_ref=z_halo.at[way, t, c],
            send_sem=z_send.at[way, c],
            recv_sem=z_recv.at[way, t, c],
            device_id={"grp": g + 1 - 2 * way},
            device_id_type=MESH,
        )

    def sending(axis, way):
        return has[axis][1 - way]

    def receiving(axis, way):
        return has[axis][way]

    pl.semaphore_wait(barrier, n_slab - 1 + n_grp - 1)

    def send_first(c):
        for way in range(2):

            @pl.when(sending(0, way))
            def _(way=way):
                x_first(c, way).start()

    for c in range(GROUP):
        send_first(c)

    def pack(values):
        packed = jnp.zeros((8, 128), jnp.float32)
        for i, value in enumerate(values):
            packed = jnp.where(
                lane_slot == i, pltpu.roll(value, (4 + 8 * i) % 128, 1), packed
            )
        return packed

    stage_rows = stage.reshape(CHUNKS * CHUNK * CX * CY, CZ)
    halo_rows = first_halo.reshape(2 * CHUNKS * CHUNK * WIDTH * CY, CZ)

    def bring_in(c):
        load(c).wait()

        @pl.loop(0, CX // 2)
        def _(j):
            values = []
            for i in range(16):
                value = stage_rows[pl.ds(c * 1024 + j * 16 + i, 8, stride=CX * CY), :]
                field[0, c, WIDTH + 2 * j + i // 8, i % 8] = value
                values.append(value)
            z_own[0, c, j] = pack(values)

        for way in range(2):

            @pl.when(sending(1, way))
            def _(way=way):
                z_copy(0, c, way).start()

    @pl.loop(0, GROUP)
    def _(c):
        bring_in(c)

    weights = weight[...]

    def advance(c, t):
        for way in range(2):

            @pl.when(receiving(0, way))
            def _(way=way):
                @pl.when(t == 0)
                def _():
                    x_first(c, way).wait_recv()

                    @pl.loop(0, WIDTH)
                    def _(x):
                        for y in range(CY):
                            field[0, c, way * (CX + WIDTH) + x, y] = halo_rows[
                                pl.ds((way * CHUNKS + c) * 256 + x * 8 + y, 8, stride=WIDTH * CY), :
                            ]

                @pl.when(t > 0)
                def _():
                    x_copy(t, c, way).wait_recv()

            @pl.when(receiving(1, way))
            def _(way=way):
                z_copy(t, c, way).wait_recv()

        mine = z_own[t, c].reshape(64, 128)
        left = z_halo[0, t, c].reshape(64, 128)
        right = z_halo[1, t, c].reshape(64, 128)
        half = lax.broadcasted_iota(jnp.int32, (64, 128), 1) % 8 < WIDTH
        change = jnp.where(half, left, right) - mine
        z_fix[...] = lax.dot_general(
            change, z_map[...], (((1,), (0,)), ((), ())), precision=EXACT,
            preferred_element_type=jnp.float32,
        ).reshape(8, 8, 128)
        before = jnp.maximum(t - 1, 0)

        @pl.loop(0, CX // 2)
        def _(j):
            fix = z_fix[j]
            values = []
            for i in range(16):
                y = i % 8
                x = 2 * j + i // 8

                def at(dx, dy):
                    return field[t, c, WIDTH + x + dx, y + dy]

                center = at(0, 0)
                total = (3.0 * A0) * center
                for k in range(1, 5):
                    beside = at(k, 0) + at(-k, 0)
                    if y + k < CY:
                        beside = beside + at(0, k)
                    if y - k >= 0:
                        beside = beside + at(0, -k)
                    beside = beside + (pltpu.roll(center, k, 1) + pltpu.roll(center, CZ - k, 1))
                    total = total + A[k] * beside
                correction = pltpu.roll(fix, (128 - 4 - 8 * i) % 128, 1)
                total = total + jnp.where(edge, correction, 0.0)
                old = field[before, c, WIDTH + x, y]
                value = (2.0 * center - old) + speed[x, y] * total
                field[t + 1, c, WIDTH + x, y] = value
                latest[16 * j + i] = value
                values.append(value)

            @pl.when(t < STEPS - 1)
            def _():
                z_own[t + 1, c, j] = pack(values)

        @pl.when(t < STEPS - 1)
        def _():
            for way in range(2):

                @pl.when(sending(0, way))
                def _(way=way):
                    @pl.when(t == 0)
                    def _():
                        x_first(c, way).wait_send()

                    @pl.when(t > 0)
                    def _():
                        x_copy(t, c, way).wait_send()

                    x_copy(t + 1, c, way).start()

                @pl.when(sending(1, way))
                def _(way=way):
                    z_copy(t, c, way).wait_send()
                    z_copy(t + 1, c, way).start()

        @pl.when(t == STEPS - 1)
        def _():
            for way in range(2):

                @pl.when(sending(0, way))
                def _(way=way):
                    x_copy(t, c, way).wait_send()

                @pl.when(sending(1, way))
                def _(way=way):
                    z_copy(t, c, way).wait_send()

        found = jnp.zeros((8, 128), jnp.float32)
        for r in range(cell.shape[0]):
            where = cell[r]
            value = latest[where // CZ]
            shift = (r + CZ) - where % CZ
            value = pltpu.roll(value, shift % 128, 1)
            found = jnp.where(lane == r, value, found)
        traces[t, pl.ds(c * CHUNK, CHUNK), :] = found * weights

        @pl.when(t == STEPS - 1)
        def _():
            @pl.loop(0, CX)
            def _(x):
                for y in range(CY):
                    stage_rows[pl.ds(c * 1024 + x * 8 + y, 8, stride=CX * CY), :] = latest[x * 8 + y]

            pltpu.make_async_copy(
                stage.at[c], wave_out.at[pl.ds(c * CHUNK, CHUNK)], store_sem.at[c]
            ).start()

    @pl.loop(0, CHUNKS * STEPS)
    def _(n):
        block = n // (GROUP * STEPS)
        t = n % (GROUP * STEPS) // GROUP
        c = block * GROUP + n % GROUP
        advance(c, t)

        @pl.when((t == STEPS - 1) & (block < CHUNKS // GROUP - 1))
        def _():
            send_first(c + GROUP)
            bring_in(c + GROUP)

    gram = jnp.zeros((PROBES, PROBES), jnp.float32)
    for t in range(STEPS):
        gram = gram + dot_nt(traces[t], traces[t])
    folded = jnp.concatenate([gram[:32], gram[32:]], axis=1)

    n_y = 8
    place_y = s % n_y
    place_x = s // n_y

    def stage_copies(buffer, count, me, base, device):
        def one(k):
            return pltpu.make_async_remote_copy(
                src_ref=buffer.at[me],
                dst_ref=buffer.at[me],
                send_sem=sum_send.at[base + k],
                recv_sem=sum_recv.at[base + k],
                device_id=device(lax.rem(me + k, count)),
                device_id_type=MESH,
            )

        return [one(k) for k in range(1, count)]

    def begin(buffer, count, me, base, device, value):
        buffer[me] = value
        copies = stage_copies(buffer, count, me, base, device)
        for copy in copies:
            copy.start()
        return copies

    def finish(buffer, count, copies):
        for copy in copies:
            copy.wait_recv()
        total = buffer[0]
        for k in range(1, count):
            total = total + buffer[k]
        for copy in copies:
            copy.wait_send()
        return total

    n_x = n_slab // n_y
    copies = begin(
        sum_a, n_y, place_y, 0, lambda other: {"slab": place_x * n_y + other}, folded
    )

    recs = cell.shape[0]
    own_col = owner[...]
    r_row = lax.broadcasted_iota(jnp.int32, (recs, 128), 0)
    r_col = lax.broadcasted_iota(jnp.int32, (recs, 128), 1)
    own_row = jnp.sum(jnp.where(r_row == r_col, own_col, 0), axis=0, keepdims=True)
    same = (own_col == own_row) & (r_row < r_col)
    slot = jnp.sum(jnp.where(same, 1, 0), axis=0, keepdims=True)
    lane_row = lax.broadcasted_iota(jnp.int32, (1, 128), 1)
    target = jnp.where(lane_row < recs, own_row * CAP + slot, -1)
    spots = lax.broadcasted_iota(jnp.int32, (n_slab * CAP, 128), 0)
    placer = jnp.where(spots == target, 1.0, 0.0)
    outgoing[...] = dot_nt(placer, traces[...].reshape(STEPS * PROBES, 128)).reshape(
        n_slab, CAP, STEPS * PROBES
    )

    def to_owner(k):
        other = lax.rem(s + k, n_slab)
        return pltpu.make_async_remote_copy(
            src_ref=outgoing.at[other],
            dst_ref=incoming.at[s],
            send_sem=a2a_send.at[k],
            recv_sem=a2a_recv.at[k],
            device_id={"slab": other},
            device_id_type=MESH,
        )

    to_self = pltpu.make_async_copy(outgoing.at[s], incoming.at[s], own_sem)
    to_self.start()

    @pl.loop(1, n_slab)
    def _(k):
        to_owner(k).start()

    total = finish(sum_a, n_y, copies)
    copies = begin(
        sum_b, n_x, place_x, n_y, lambda other: {"slab": other * n_y + place_y}, total
    )
    total = finish(sum_b, n_x, copies)
    copies = begin(sum_c, n_grp, g, n_y + n_x, lambda other: {"grp": other}, total)
    total = finish(sum_c, n_grp, copies)

    low = lax.broadcasted_iota(jnp.int32, (32, 128), 1) < PROBES
    unit = lax.broadcasted_iota(jnp.int32, (PROBES, 128), 0)
    unit_lane = lax.broadcasted_iota(jnp.int32, (PROBES, 128), 1)
    left = jnp.concatenate([total, pltpu.roll(total, PROBES, 1)], axis=0)
    work = jnp.where(
        unit_lane < PROBES, left, jnp.where(unit_lane - PROBES == unit, 1.0, 0.0)
    )
    parts = [work[8 * b : 8 * b + 8] for b in range(8)]
    sub = lax.broadcasted_iota(jnp.int32, (8, 128), 0)
    for k in range(PROBES):
        b0 = k // 8
        pivot_row = parts[b0][k % 8 : k % 8 + 1, :]
        scaled = pivot_row / pivot_row[:, k : k + 1]
        for b in range(b0, 8):
            factor = parts[b][:, k : k + 1]
            if b == b0:
                factor = jnp.where(sub > k % 8, factor, 0.0)
            parts[b] = parts[b] - factor * scaled
    work = jnp.concatenate(parts, axis=0)
    diag = jnp.sum(jnp.where(unit == unit_lane, work, 0.0), axis=1, keepdims=True)
    work = work * (1.0 / jnp.sqrt(diag))
    rows = n_slab * n_grp * recs * STEPS
    upper = jnp.where((unit_lane >= unit) & (unit_lane < PROBES), work, 0.0)
    r_out[...] = upper[:, :PROBES] * (1.0 / math.sqrt(rows))
    inverse = jnp.where(unit_lane >= PROBES, work, 0.0) * math.sqrt(rows)
    pair = jnp.concatenate([pltpu.roll(inverse, PROBES, 1), inverse], axis=0)

    to_self.wait()

    @pl.loop(1, n_slab)
    def _(k):
        to_owner(k).wait()

    for half in range(2):
        block = incoming[:, :, pl.ds(128 * half, 128)].reshape(n_slab * CAP, 128)
        q_out[:, pl.ds(128 * half, 128)] = dot_nt(block, pair)

    for c in range(CHUNKS):
        pltpu.make_async_copy(
            stage.at[c], wave_out.at[pl.ds(c * CHUNK, CHUNK)], store_sem.at[c]
        ).wait()


def solution(mesh):
    n_grp = mesh.shape["grp"]
    n_slab = mesh.shape["slab"]

    def per_device(probes, courant, rec_cell, rec_owner, trace_weight):
        recs = rec_cell.shape[0]
        f32 = jnp.float32
        weight = jnp.pad(trace_weight, (0, 128 - recs)).reshape(1, 128)
        vmem = pl.BlockSpec(memory_space=pltpu.VMEM)
        wave, q_basis, r_factor = pl.pallas_call(
            functools.partial(kernel, n_grp, n_slab),
            out_shape=(
                jax.ShapeDtypeStruct((PROBES, CX * CY, CZ), f32),
                jax.ShapeDtypeStruct((n_slab * CAP, STEPS * PROBES), f32),
                jax.ShapeDtypeStruct((PROBES, PROBES), f32),
            ),
            in_specs=[
                pl.BlockSpec(memory_space=pl.ANY),
                vmem,
                pl.BlockSpec(memory_space=pltpu.SMEM),
                vmem,
                vmem,
            ],
            out_specs=(pl.BlockSpec(memory_space=pl.ANY), vmem, vmem),
            scratch_shapes=[
                pltpu.VMEM((CHUNKS, CHUNK, CX * CY, CZ), f32),
                pltpu.VMEM((2, CHUNKS, CHUNK, WIDTH * CY, CZ), f32),
                pltpu.VMEM((STEPS + 1, CHUNKS, CX + 2 * WIDTH, CY, CHUNK, CZ), f32),
                pltpu.VMEM((CX * CY, CHUNK, CZ), f32),
                pltpu.VMEM((CX, CY, 8, CZ), f32),
                pltpu.VMEM((STEPS, CHUNKS, 8, 8, 128), f32),
                pltpu.VMEM((2, STEPS, CHUNKS, 8, 8, 128), f32),
                pltpu.VMEM((8, 8, 128), f32),
                pltpu.VMEM((128, 128), f32),
                pltpu.VMEM((STEPS, PROBES, 128), f32),
                pltpu.VMEM((n_slab, CAP, STEPS * PROBES), f32),
                pltpu.VMEM((n_slab, CAP, STEPS * PROBES), f32),
                pltpu.VMEM((8, 32, 128), f32),
                pltpu.VMEM((n_slab // 8, 32, 128), f32),
                pltpu.VMEM((n_grp, 32, 128), f32),
                pltpu.SemaphoreType.DMA((CHUNKS,)),
                pltpu.SemaphoreType.DMA((CHUNKS,)),
                pltpu.SemaphoreType.DMA((2, CHUNKS)),
                pltpu.SemaphoreType.DMA((2, STEPS, CHUNKS)),
                pltpu.SemaphoreType.DMA((2, CHUNKS)),
                pltpu.SemaphoreType.DMA((2, STEPS, CHUNKS)),
                pltpu.SemaphoreType.DMA((n_slab,)),
                pltpu.SemaphoreType.DMA((n_slab,)),
                pltpu.SemaphoreType.DMA,
                pltpu.SemaphoreType.DMA((8 + n_slab // 8 + n_grp,)),
                pltpu.SemaphoreType.DMA((8 + n_slab // 8 + n_grp,)),
            ],
            compiler_params=pltpu.CompilerParams(
                collective_id=0, has_side_effects=True, vmem_limit_bytes=56 * 1024 * 1024
            ),
        )(
            probes.reshape(PROBES, CX * CY, CZ),
            courant,
            rec_cell,
            rec_owner,
            weight,
        )
        return (wave.reshape(PROBES, CX, CY, CZ), q_basis, r_factor)

    return jax.shard_map(
        per_device,
        mesh=mesh,
        in_specs=(
            P(None, "slab", None, "grp"),
            P("slab", None, "grp"),
            P(("grp", "slab")),
            P(("grp", "slab"), None),
            P(("grp", "slab")),
        ),
        out_specs=(P(None, "slab", None, "grp"), P(("grp", "slab"), None), P()),
        check_vma=False,
    )
```

time: 832 us -> 154 us (0.19)
  other arithmetic: 481 us -> 0 us
  Pallas kernels: 0 us -> 145 us
  waiting for transfers between devices: 95.1 us -> 0 us
  local copies, waits for them, and re-layouts: 101 us -> 8.59 us
  blocking collectives: 70.9 us -> 0 us
  starting transfers between devices: 52.9 us -> 0 us
  matrix products: 22.8 us -> 0 us
    add x4 -> x0, other arithmetic: 356 us -> none  [per_device(): advanced = 2.0 * current - previous + speed * laplace(pad_middle(extended))]
    pallas_call x0 -> x1, Pallas kernels: none -> 145 us  [per_device(): pl.pallas_call(functools.partial(kernel, n_grp, n_slab), out_shape=(jax.S...]
    concatenate x12 -> x0, other arithmetic: 112 us -> none  [with_halo(): block = jnp.concatenate([low, block, high], axis=dim)]
    ppermute x16 -> x0, waiting for transfers between devices: 93 us -> none  [the longest x8 69.3 us: with_halo(): lax.ppermute(lax.slice_in_dim(block, block.shape[dim] - width, None, axis...]
    psum x1 -> x0, blocking collectives: 70.9 us -> none  [per_device(): lower = jnp.linalg.cholesky(lax.psum(gram, ('grp', 'slab')))]
    slice x10 -> x0, local copies, waits for them, and re-layouts: 54.8 us -> none  [the longest x7 43.7 us: with_halo(): lax.slice_in_dim(block, 0, width, axis=dim)]
    ppermute x16 -> x0, starting transfers between devices: 47.5 us -> none  [the longest x8 33.6 us: with_halo(): lax.ppermute(lax.slice_in_dim(block, block.shape[dim] - width, None, axis...]
    ppermute x8 -> x0, local copies, waits for them, and re-layouts: 36.4 us -> none  [the longest x4 18.4 us: with_halo(): lax.ppermute(lax.slice_in_dim(block, 0, width, axis=dim), axis, backward)]
  transfers between devices with their start and end apart: 17 -> 0, of which waited for: 11 -> 0; matrix products, arithmetic and copies ran while one was open for 6% -> 0% of each run, Pallas kernels for 0% -> 0%
where the time goes in v1:
time: 154 us
  Pallas kernels  145 us (94%)
  local copies, waits for them, and re-layouts  8.59 us (6%)
    pallas_call x1, Pallas kernels, per_device(): pl.pallas_call(functools.partial(kernel, n_grp, n_slab), out_shape=(jax.S...  145 us
    unnamed x8, local copies, waits for them, and re-layouts  7.42 us

profile of v1, /device:TPU:1, one launch (start us, length us, event | category | flops | bytes accessed | tf_op | source)
XLA Modules:
  0.0 153.7 jit_solution(17600544119357539384)
XLA Ops:
  0.6 1.2 pad_bitcast_fusion.weight
  1.8 1.4 copy.8.owner
  3.2 144.5 %shard_map.76 = (f32[64,128,128]{2,1,0:T(8,128)}, f32[256,256]{1,0:T(8,128)}, f32[64,64]{1,0:T(8,128)}) custom-call(f32[64,128,128]{2,1,0:T(8,128)} %bitcast.4, f32[16,8,128]{2,1,0:T(8,128)} %courant.1, s32[64]{0:T(128)} %cell.1, s32[64,1]{1,0:T(8,128)} %copy.8.owner, f32[1,128]{1,0:T(1,128)} %pad_bitcast_fusion.weight), custom_call_target="tpu_custom_call" | custom-call | tf_op jit(solution)/shard_map/pallas_call | solution.py:489
  147.7 0.0 copy-start
  147.7 0.0 copy-start.1
  147.7 4.7 %copy.12 = f32[64,16,8,128]{3,2,1,0:T(8,128)} copy(f32[64,16,8,128]{3,2,1,0:T(8,128)} %bitcast.5) | data formatting | bytes 8388608
  152.4 0.0 copy-done
  152.4 0.7 copy.13
  153.1 0.0 copy-done.1
  153.1 0.6 copy.14
Async XLA Ops:
  147.7 4.8 %copy-start = (f32[256,256]{1,0:T(8,128)S(1)}, f32[256,256]{1,0:T(8,128)}, u32[]{:S(2)}) copy-start(f32[256,256]{1,0:T(8,128)} %get-tuple-element.13) | copy-start | bytes 786436
  147.7 5.5 %copy-start.1 = (f32[64,64]{1,0:T(8,128)S(1)}, f32[64,64]{1,0:T(8,128)}, u32[]{:S(2)}) copy-start(f32[64,64]{1,0:T(8,128)} %get-tuple-element.14) | copy-start | bytes 49156

commit v2 on v1

--- a/solution.py
+++ b/solution.py
@@ -7,6 +7,8 @@
 from jax.experimental import pallas as pl
 from jax.experimental.pallas import tpu as pltpu
 from jax.sharding import PartitionSpec as P
+import numpy as np
+import ml_dtypes
 
 PROBES = 64
 CX = 16
@@ -25,6 +27,26 @@
 A = (0.0, 8.0 / 5.0, -1.0 / 5.0, 8.0 / 315.0, -1.0 / 560.0)
 
 
+def halves(value):
+    high = float(np.float32(value).astype(ml_dtypes.bfloat16))
+    low = float(np.float32(value - high).astype(ml_dtypes.bfloat16))
+    return high, low
+
+
+def banded(gap, low_part, coefficients):
+    table = jnp.zeros(gap.shape, jnp.float32)
+    for k, value in enumerate(coefficients):
+        high, low = halves(value)
+        table = jnp.where(gap == k, jnp.where(low_part, low, high), table)
+    return table
+
+
+def split(value):
+    high = value.astype(jnp.bfloat16)
+    low = (value - high.astype(jnp.float32)).astype(jnp.bfloat16)
+    return high, low
+
+
 def dot_nt(a, b):
     return lax.dot_general(
         a, b, (((1,), (1,)), ((), ())), precision=EXACT, preferred_element_type=jnp.float32
@@ -42,9 +64,11 @@
     wave_out,
     q_out,
     r_out,
-    stage,
-    first_halo,
     field,
+    parts_of,
+    z_band,
+    row_of,
+    turn_of,
     latest,
     speed,
     z_own,
@@ -73,13 +97,18 @@
     g = lax.axis_index("grp")
     has = ((s > 0, s < n_slab - 1), (g > 0, g < n_grp - 1))
 
-    def load(c):
+    def load(c, p):
         return pltpu.make_async_copy(
-            probes.at[pl.ds(c * CHUNK, CHUNK)], stage.at[c], load_sem.at[c]
-        )
+            probes.at[c * CHUNK + p], field.at[0, c, pl.ds(WIDTH, CX), :, p], load_sem.at[c]
+        )
+
+    def loaded(c):
+        whole = field.at[0, c, pl.ds(WIDTH, CX)]
+        return pltpu.make_async_copy(whole, whole, load_sem.at[c])
 
     for c in range(CHUNKS):
-        load(c).start()
+        for p in range(CHUNK):
+            load(c, p).start()
 
     barrier = pltpu.get_barrier_semaphore()
 
@@ -100,14 +129,24 @@
     lane_slot = lane // 8
     low_half = (lane % 8) < WIDTH
 
-    row_i = lax.broadcasted_iota(jnp.int32, (128, 128), 0)
-    col_i = lax.broadcasted_iota(jnp.int32, (128, 128), 1)
+    row_i = lax.broadcasted_iota(jnp.int32, (256, 256), 0) % 128
+    col_i = lax.broadcasted_iota(jnp.int32, (256, 256), 1)
+    low_part = col_i >= 128
+    col_i = col_i % 128
     gap = jnp.abs(row_i - col_i)
     crossing = (row_i // 8 == col_i // 8) & ((row_i % 8 < WIDTH) != (col_i % 8 < WIDTH))
-    table = jnp.zeros((128, 128), jnp.float32)
-    for k in range(1, 5):
-        table = jnp.where(gap == k, A[k], table)
-    z_map[...] = jnp.where(crossing, table, 0.0)
+    z_band[...] = banded(gap, low_part, (3.0 * A0,) + A[1:]).astype(jnp.bfloat16)
+    z_map[...] = jnp.where(crossing, banded(gap, low_part, A), 0.0).astype(jnp.bfloat16)
+
+    recs = cell.shape[0]
+
+    @pl.loop(0, recs)
+    def _(r):
+        where = cell[r]
+        row_of[r] = where // CZ
+        turn_of[r] = (r + CZ - where % CZ) % CZ
+
+    latest[...] = jnp.zeros(latest.shape, jnp.float32)
 
     @pl.loop(0, CX)
     def _(x):
@@ -132,16 +171,6 @@
                 @pl.loop(0, CHUNKS)
                 def _(c):
                     z_halo[side, t, c] = jnp.zeros((8, 8, 128), jnp.float32)
-
-    def x_first(c, way):
-        return pltpu.make_async_remote_copy(
-            src_ref=probes.at[pl.ds(c * CHUNK, CHUNK), pl.ds((1 - way) * (CX - WIDTH) * CY, WIDTH * CY)],
-            dst_ref=first_halo.at[way, c],
-            send_sem=x_send.at[way, c],
-            recv_sem=x_recv.at[way, 0, c],
-            device_id={"slab": s + 1 - 2 * way},
-            device_id_type=MESH,
-        )
 
     def x_copy(t, c, way):
         return pltpu.make_async_remote_copy(
@@ -155,7 +184,7 @@
 
     def z_copy(t, c, way):
         return pltpu.make_async_remote_copy(
-            src_ref=z_own.at[t, c],
+            src_ref=z_own.at[t, c, pl.ds(1, 8)],
             dst_ref=z_halo.at[way, t, c],
             send_sem=z_send.at[way, c],
             recv_sem=z_recv.at[way, t, c],
@@ -170,16 +199,6 @@
         return has[axis][way]
 
     pl.semaphore_wait(barrier, n_slab - 1 + n_grp - 1)
-
-    def send_first(c):
-        for way in range(2):
-
-            @pl.when(sending(0, way))
-            def _(way=way):
-                x_first(c, way).start()
-
-    for c in range(GROUP):
-        send_first(c)
 
     def pack(values):
         packed = jnp.zeros((8, 128), jnp.float32)
@@ -189,20 +208,26 @@
             )
         return packed
 
-    stage_rows = stage.reshape(CHUNKS * CHUNK * CX * CY, CZ)
-    halo_rows = first_halo.reshape(2 * CHUNKS * CHUNK * WIDTH * CY, CZ)
+    def keep_parts(c, j, values):
+        for i in range(0, 16, 2):
+            high, low = split(jnp.concatenate(values[i : i + 2], axis=0))
+            spot = pl.ds(pl.multiple_of(128 * j + 8 * i, 16), 16)
+            parts_of[c, spot, pl.ds(0, 128)] = high
+            parts_of[c, spot, pl.ds(128, 128)] = low
 
     def bring_in(c):
-        load(c).wait()
+        loaded(c).wait()
+        for way in range(2):
+
+            @pl.when(sending(0, way))
+            def _(way=way):
+                x_copy(0, c, way).start()
 
         @pl.loop(0, CX // 2)
         def _(j):
-            values = []
-            for i in range(16):
-                value = stage_rows[pl.ds(c * 1024 + j * 16 + i, 8, stride=CX * CY), :]
-                field[0, c, WIDTH + 2 * j + i // 8, i % 8] = value
-                values.append(value)
-            z_own[0, c, j] = pack(values)
+            values = [field[0, c, WIDTH + 2 * j + i // 8, i % 8] for i in range(16)]
+            z_own[0, c, j + 1] = pack(values)
+            keep_parts(c, j, values)
 
         for way in range(2):
 
@@ -214,46 +239,48 @@
     def _(c):
         bring_in(c)
 
-    weights = weight[...]
+    weights = jnp.zeros((1, 128), jnp.float32)
+    for r in range(recs):
+        weights = jnp.where(lane[:1] == r, weight[r], weights)
+
+    def store(c, p):
+        return pltpu.make_async_copy(
+            field.at[STEPS, c, pl.ds(WIDTH, CX), :, p], wave_out.at[c * CHUNK + p], store_sem.at[c]
+        )
 
     def advance(c, t):
         for way in range(2):
 
             @pl.when(receiving(0, way))
             def _(way=way):
-                @pl.when(t == 0)
-                def _():
-                    x_first(c, way).wait_recv()
-
-                    @pl.loop(0, WIDTH)
-                    def _(x):
-                        for y in range(CY):
-                            field[0, c, way * (CX + WIDTH) + x, y] = halo_rows[
-                                pl.ds((way * CHUNKS + c) * 256 + x * 8 + y, 8, stride=WIDTH * CY), :
-                            ]
-
-                @pl.when(t > 0)
-                def _():
-                    x_copy(t, c, way).wait_recv()
+                x_copy(t, c, way).wait_recv()
 
             @pl.when(receiving(1, way))
             def _(way=way):
                 z_copy(t, c, way).wait_recv()
 
-        mine = z_own[t, c].reshape(64, 128)
         left = z_halo[0, t, c].reshape(64, 128)
         right = z_halo[1, t, c].reshape(64, 128)
         half = lax.broadcasted_iota(jnp.int32, (64, 128), 1) % 8 < WIDTH
-        change = jnp.where(half, left, right) - mine
-        z_fix[...] = lax.dot_general(
-            change, z_map[...], (((1,), (0,)), ((), ())), precision=EXACT,
-            preferred_element_type=jnp.float32,
-        ).reshape(8, 8, 128)
+        high, low = split(jnp.where(half, left, right))
+        both = jnp.dot(
+            jnp.concatenate([high, low], axis=1), z_map[...], preferred_element_type=jnp.float32
+        )
+        z_fix[...] = (both[:, :128] + both[:, 128:]).reshape(8, 8, 128)
         before = jnp.maximum(t - 1, 0)
 
         @pl.loop(0, CX // 2)
         def _(j):
             fix = z_fix[j]
+            earlier = pl.multiple_of(16 * jnp.maximum(j - 1, 0), 16)
+
+            @pl.when(t < STEPS - 1)
+            def _():
+                z_own[t + 1, c, j] = pack([latest[earlier + i] for i in range(16)])
+
+            rows = parts_of[c, pl.ds(pl.multiple_of(128 * j, 128), 128), :]
+            both = jnp.dot(rows, z_band[...], preferred_element_type=jnp.float32)
+            along_z = both[:, :128] + both[:, 128:]
             values = []
             for i in range(16):
                 y = i % 8
@@ -263,14 +290,13 @@
                     return field[t, c, WIDTH + x + dx, y + dy]
 
                 center = at(0, 0)
-                total = (3.0 * A0) * center
+                total = along_z[8 * i : 8 * i + 8]
                 for k in range(1, 5):
                     beside = at(k, 0) + at(-k, 0)
                     if y + k < CY:
                         beside = beside + at(0, k)
                     if y - k >= 0:
                         beside = beside + at(0, -k)
-                    beside = beside + (pltpu.roll(center, k, 1) + pltpu.roll(center, CZ - k, 1))
                     total = total + A[k] * beside
                 correction = pltpu.roll(fix, (128 - 4 - 8 * i) % 128, 1)
                 total = total + jnp.where(edge, correction, 0.0)
@@ -280,24 +306,16 @@
                 latest[16 * j + i] = value
                 values.append(value)
 
-            @pl.when(t < STEPS - 1)
-            def _():
-                z_own[t + 1, c, j] = pack(values)
+            keep_parts(c, j, values)
 
         @pl.when(t < STEPS - 1)
         def _():
+            z_own[t + 1, c, 8] = pack([latest[112 + i] for i in range(16)])
             for way in range(2):
 
                 @pl.when(sending(0, way))
                 def _(way=way):
-                    @pl.when(t == 0)
-                    def _():
-                        x_first(c, way).wait_send()
-
-                    @pl.when(t > 0)
-                    def _():
-                        x_copy(t, c, way).wait_send()
-
+                    x_copy(t, c, way).wait_send()
                     x_copy(t + 1, c, way).start()
 
                 @pl.when(sending(1, way))
@@ -318,24 +336,15 @@
                     z_copy(t, c, way).wait_send()
 
         found = jnp.zeros((8, 128), jnp.float32)
-        for r in range(cell.shape[0]):
-            where = cell[r]
-            value = latest[where // CZ]
-            shift = (r + CZ) - where % CZ
-            value = pltpu.roll(value, shift % 128, 1)
+        for r in range(recs):
+            value = pltpu.roll(latest[row_of[r]], turn_of[r], 1)
             found = jnp.where(lane == r, value, found)
         traces[t, pl.ds(c * CHUNK, CHUNK), :] = found * weights
 
         @pl.when(t == STEPS - 1)
         def _():
-            @pl.loop(0, CX)
-            def _(x):
-                for y in range(CY):
-                    stage_rows[pl.ds(c * 1024 + x * 8 + y, 8, stride=CX * CY), :] = latest[x * 8 + y]
-
-            pltpu.make_async_copy(
-                stage.at[c], wave_out.at[pl.ds(c * CHUNK, CHUNK)], store_sem.at[c]
-            ).start()
+            for p in range(CHUNK):
+                store(c, p).start()
 
     @pl.loop(0, CHUNKS * STEPS)
     def _(n):
@@ -346,7 +355,6 @@
 
         @pl.when((t == STEPS - 1) & (block < CHUNKS // GROUP - 1))
         def _():
-            send_first(c + GROUP)
             bring_in(c + GROUP)
 
     gram = jnp.zeros((PROBES, PROBES), jnp.float32)
@@ -393,13 +401,12 @@
         sum_a, n_y, place_y, 0, lambda other: {"slab": place_x * n_y + other}, folded
     )
 
-    recs = cell.shape[0]
-    own_col = owner[...]
-    r_row = lax.broadcasted_iota(jnp.int32, (recs, 128), 0)
-    r_col = lax.broadcasted_iota(jnp.int32, (recs, 128), 1)
-    own_row = jnp.sum(jnp.where(r_row == r_col, own_col, 0), axis=0, keepdims=True)
-    same = (own_col == own_row) & (r_row < r_col)
-    slot = jnp.sum(jnp.where(same, 1, 0), axis=0, keepdims=True)
+    own_row = jnp.zeros((1, 128), jnp.int32)
+    for r in range(recs):
+        own_row = jnp.where(lane[:1] == r, owner[r], own_row)
+    slot = jnp.zeros((1, 128), jnp.int32)
+    for r in range(recs):
+        slot = slot + jnp.where((own_row == owner[r]) & (lane[:1] > r), 1, 0)
     lane_row = lax.broadcasted_iota(jnp.int32, (1, 128), 1)
     target = jnp.where(lane_row < recs, own_row * CAP + slot, -1)
     spots = lax.broadcasted_iota(jnp.int32, (n_slab * CAP, 128), 0)
@@ -472,9 +479,8 @@
         q_out[:, pl.ds(128 * half, 128)] = dot_nt(block, pair)
 
     for c in range(CHUNKS):
-        pltpu.make_async_copy(
-            stage.at[c], wave_out.at[pl.ds(c * CHUNK, CHUNK)], store_sem.at[c]
-        ).wait()
+        whole = field.at[STEPS, c, pl.ds(WIDTH, CX)]
+        pltpu.make_async_copy(whole, whole, store_sem.at[c]).wait()
 
 
 def solution(mesh):
@@ -484,33 +490,35 @@
     def per_device(probes, courant, rec_cell, rec_owner, trace_weight):
         recs = rec_cell.shape[0]
         f32 = jnp.float32
-        weight = jnp.pad(trace_weight, (0, 128 - recs)).reshape(1, 128)
+        smem = pl.BlockSpec(memory_space=pltpu.SMEM)
         vmem = pl.BlockSpec(memory_space=pltpu.VMEM)
         wave, q_basis, r_factor = pl.pallas_call(
             functools.partial(kernel, n_grp, n_slab),
             out_shape=(
-                jax.ShapeDtypeStruct((PROBES, CX * CY, CZ), f32),
+                jax.ShapeDtypeStruct((PROBES, CX, CY, CZ), f32),
                 jax.ShapeDtypeStruct((n_slab * CAP, STEPS * PROBES), f32),
                 jax.ShapeDtypeStruct((PROBES, PROBES), f32),
             ),
             in_specs=[
                 pl.BlockSpec(memory_space=pl.ANY),
                 vmem,
-                pl.BlockSpec(memory_space=pltpu.SMEM),
-                vmem,
-                vmem,
+                smem,
+                smem,
+                smem,
             ],
             out_specs=(pl.BlockSpec(memory_space=pl.ANY), vmem, vmem),
             scratch_shapes=[
-                pltpu.VMEM((CHUNKS, CHUNK, CX * CY, CZ), f32),
-                pltpu.VMEM((2, CHUNKS, CHUNK, WIDTH * CY, CZ), f32),
                 pltpu.VMEM((STEPS + 1, CHUNKS, CX + 2 * WIDTH, CY, CHUNK, CZ), f32),
+                pltpu.VMEM((CHUNKS, CX * CY * CHUNK, 2 * CZ), jnp.bfloat16),
+                pltpu.VMEM((2 * CZ, 2 * CZ), jnp.bfloat16),
+                pltpu.SMEM((recs,), jnp.int32),
+                pltpu.SMEM((recs,), jnp.int32),
                 pltpu.VMEM((CX * CY, CHUNK, CZ), f32),
                 pltpu.VMEM((CX, CY, 8, CZ), f32),
-                pltpu.VMEM((STEPS, CHUNKS, 8, 8, 128), f32),
+                pltpu.VMEM((STEPS, CHUNKS, 9, 8, 128), f32),
                 pltpu.VMEM((2, STEPS, CHUNKS, 8, 8, 128), f32),
                 pltpu.VMEM((8, 8, 128), f32),
-                pltpu.VMEM((128, 128), f32),
+                pltpu.VMEM((256, 256), jnp.bfloat16),
                 pltpu.VMEM((STEPS, PROBES, 128), f32),
                 pltpu.VMEM((n_slab, CAP, STEPS * PROBES), f32),
                 pltpu.VMEM((n_slab, CAP, STEPS * PROBES), f32),
@@ -533,13 +541,13 @@
                 collective_id=0, has_side_effects=True, vmem_limit_bytes=56 * 1024 * 1024
             ),
         )(
-            probes.reshape(PROBES, CX * CY, CZ),
+            probes,
             courant,
             rec_cell,
-            rec_owner,
-            weight,
-        )
-        return (wave.reshape(PROBES, CX, CY, CZ), q_basis, r_factor)
+            rec_owner.reshape(recs),
+            trace_weight,
+        )
+        return (wave, q_basis, r_factor)
 
     return jax.shard_map(
         per_device,

time: 154 us -> 142 us (0.922)
  Pallas kernels: 145 us -> 135 us
  local copies, waits for them, and re-layouts: 8.59 us -> 6.06 us
    pallas_call x1, Pallas kernels: 145 us -> 135 us  [per_device(): pl.pallas_call(functools.partial(kernel, n_grp, n_slab), out_shape=(jax.S...]
    unnamed x8 -> x7, local copies, waits for them, and re-layouts: 7.42 us -> 6.06 us
where the time goes in v2:
time: 142 us
  Pallas kernels  135 us (95%)
  local copies, waits for them, and re-layouts  6.06 us (4%)
    pallas_call x1, Pallas kernels, per_device(): pl.pallas_call(functools.partial(kernel, n_grp, n_slab), out_shape=(jax.S...  135 us
    unnamed x7, local copies, waits for them, and re-layouts  6.06 us

profile of v2, /device:TPU:1, one launch (start us, length us, event | category | flops | bytes accessed | tf_op | source)
XLA Modules:
  0.0 141.8 jit_solution(1410231710721700890)
XLA Ops:
  0.6 135.1 %shard_map.76 = (f32[64,16,8,128]{3,2,1,0:T(8,128)}, f32[256,256]{1,0:T(8,128)}, f32[64,64]{1,0:T(8,128)}) custom-call(f32[64,16,8,128]{3,2,1,0:T(8,128)} %probes.1, f32[16,8,128]{2,1,0:T(8,128)} %courant.1, s32[64]{0:T(128)} %cell.1, s32[64]{0:T(128)} %bitcast.1, f32[64]{0:T(128)} %weight.1), custom_call_target="tpu_custom_call" | custom-call | tf_op jit(solution)/shard_map/pallas_call | solution.py:495
  135.7 0.0 copy-start
  135.7 0.0 copy-start.1
  135.7 4.7 %copy.11 = f32[64,16,8,128]{3,2,1,0:T(8,128)} copy(f32[64,16,8,128]{3,2,1,0:T(8,128)} %get-tuple-element.6) | data formatting | bytes 8388608
  140.5 0.0 copy-done
  140.5 0.7 copy.12
  141.2 0.0 copy-done.1
  141.2 0.6 copy.13
Async XLA Ops:
  135.7 4.8 %copy-start = (f32[256,256]{1,0:T(8,128)S(1)}, f32[256,256]{1,0:T(8,128)}, u32[]{:S(2)}) copy-start(f32[256,256]{1,0:T(8,128)} %get-tuple-element.7) | copy-start | bytes 786436
  135.7 5.5 %copy-start.1 = (f32[64,64]{1,0:T(8,128)S(1)}, f32[64,64]{1,0:T(8,128)}, u32[]{:S(2)}) copy-start(f32[64,64]{1,0:T(8,128)} %get-tuple-element.8) | copy-start | bytes 49156

commit v3 on v2

--- a/solution.py
+++ b/solution.py
@@ -64,9 +64,14 @@
     wave_out,
     q_out,
     r_out,
-    field,
+    field_0,
+    field_1,
+    field_2,
+    field_3,
+    field_4,
     parts_of,
     z_band,
+    z_lap,
     row_of,
     turn_of,
     latest,
@@ -93,17 +98,18 @@
     sum_send,
     sum_recv,
 ):
+    field = (field_0, field_1, field_2, field_3, field_4)
     s = lax.axis_index("slab")
     g = lax.axis_index("grp")
     has = ((s > 0, s < n_slab - 1), (g > 0, g < n_grp - 1))
 
     def load(c, p):
         return pltpu.make_async_copy(
-            probes.at[c * CHUNK + p], field.at[0, c, pl.ds(WIDTH, CX), :, p], load_sem.at[c]
+            probes.at[c * CHUNK + p], field[0].at[c, pl.ds(WIDTH, CX), :, p], load_sem.at[c]
         )
 
     def loaded(c):
-        whole = field.at[0, c, pl.ds(WIDTH, CX)]
+        whole = field[0].at[c, pl.ds(WIDTH, CX)]
         return pltpu.make_async_copy(whole, whole, load_sem.at[c])
 
     for c in range(CHUNKS):
@@ -158,11 +164,10 @@
 
         @pl.when(jnp.logical_not(has[0][side]))
         def _(side=side):
-            @pl.loop(0, STEPS)
-            def _(t):
-                @pl.loop(0, CHUNKS)
-                def _(c):
-                    field[t, c, pl.ds(side * (CX + WIDTH), WIDTH)] = blank
+            @pl.loop(0, CHUNKS)
+            def _(c):
+                for t in range(STEPS):
+                    field[t][c, pl.ds(side * (CX + WIDTH), WIDTH)] = blank
 
         @pl.when(jnp.logical_not(has[1][side]))
         def _(side=side):
@@ -174,8 +179,8 @@
 
     def x_copy(t, c, way):
         return pltpu.make_async_remote_copy(
-            src_ref=field.at[t, c, pl.ds(WIDTH + (1 - way) * (CX - WIDTH), WIDTH)],
-            dst_ref=field.at[t, c, pl.ds(way * (CX + WIDTH), WIDTH)],
+            src_ref=field[t].at[c, pl.ds(WIDTH + (1 - way) * (CX - WIDTH), WIDTH)],
+            dst_ref=field[t].at[c, pl.ds(way * (CX + WIDTH), WIDTH)],
             send_sem=x_send.at[way, c],
             recv_sem=x_recv.at[way, t, c],
             device_id={"slab": s + 1 - 2 * way},
@@ -225,7 +230,7 @@
 
         @pl.loop(0, CX // 2)
         def _(j):
-            values = [field[0, c, WIDTH + 2 * j + i // 8, i % 8] for i in range(16)]
+            values = [field[0][c, WIDTH + 2 * j + i // 8, i % 8] for i in range(16)]
             z_own[0, c, j + 1] = pack(values)
             keep_parts(c, j, values)
 
@@ -245,7 +250,7 @@
 
     def store(c, p):
         return pltpu.make_async_copy(
-            field.at[STEPS, c, pl.ds(WIDTH, CX), :, p], wave_out.at[c * CHUNK + p], store_sem.at[c]
+            field[STEPS].at[c, pl.ds(WIDTH, CX), :, p], wave_out.at[c * CHUNK + p], store_sem.at[c]
         )
 
     def advance(c, t):
@@ -267,27 +272,26 @@
             jnp.concatenate([high, low], axis=1), z_map[...], preferred_element_type=jnp.float32
         )
         z_fix[...] = (both[:, :128] + both[:, 128:]).reshape(8, 8, 128)
-        before = jnp.maximum(t - 1, 0)
+        before = max(t - 1, 0)
+        both = jnp.dot(parts_of[c], z_band[...], preferred_element_type=jnp.float32)
+        z_lap[...] = both[:, :128] + both[:, 128:]
 
         @pl.loop(0, CX // 2)
         def _(j):
             fix = z_fix[j]
             earlier = pl.multiple_of(16 * jnp.maximum(j - 1, 0), 16)
 
-            @pl.when(t < STEPS - 1)
-            def _():
+            if t < STEPS - 1:
                 z_own[t + 1, c, j] = pack([latest[earlier + i] for i in range(16)])
 
-            rows = parts_of[c, pl.ds(pl.multiple_of(128 * j, 128), 128), :]
-            both = jnp.dot(rows, z_band[...], preferred_element_type=jnp.float32)
-            along_z = both[:, :128] + both[:, 128:]
+            along_z = z_lap[pl.ds(pl.multiple_of(128 * j, 128), 128), :]
             values = []
             for i in range(16):
                 y = i % 8
                 x = 2 * j + i // 8
 
                 def at(dx, dy):
-                    return field[t, c, WIDTH + x + dx, y + dy]
+                    return field[t][c, WIDTH + x + dx, y + dy]
 
                 center = at(0, 0)
                 total = along_z[8 * i : 8 * i + 8]
@@ -300,16 +304,16 @@
                     total = total + A[k] * beside
                 correction = pltpu.roll(fix, (128 - 4 - 8 * i) % 128, 1)
                 total = total + jnp.where(edge, correction, 0.0)
-                old = field[before, c, WIDTH + x, y]
+                old = field[before][c, WIDTH + x, y]
                 value = (2.0 * center - old) + speed[x, y] * total
-                field[t + 1, c, WIDTH + x, y] = value
+                field[t + 1][c, WIDTH + x, y] = value
                 latest[16 * j + i] = value
                 values.append(value)
 
-            keep_parts(c, j, values)
-
-        @pl.when(t < STEPS - 1)
-        def _():
+            if t < STEPS - 1:
+                keep_parts(c, j, values)
+
+        if t < STEPS - 1:
             z_own[t + 1, c, 8] = pack([latest[112 + i] for i in range(16)])
             for way in range(2):
 
@@ -323,8 +327,7 @@
                     z_copy(t, c, way).wait_send()
                     z_copy(t + 1, c, way).start()
 
-        @pl.when(t == STEPS - 1)
-        def _():
+        if t == STEPS - 1:
             for way in range(2):
 
                 @pl.when(sending(0, way))
@@ -341,21 +344,23 @@
             found = jnp.where(lane == r, value, found)
         traces[t, pl.ds(c * CHUNK, CHUNK), :] = found * weights
 
-        @pl.when(t == STEPS - 1)
-        def _():
+        if t == STEPS - 1:
             for p in range(CHUNK):
                 store(c, p).start()
 
-    @pl.loop(0, CHUNKS * STEPS)
-    def _(n):
-        block = n // (GROUP * STEPS)
-        t = n % (GROUP * STEPS) // GROUP
-        c = block * GROUP + n % GROUP
-        advance(c, t)
-
-        @pl.when((t == STEPS - 1) & (block < CHUNKS // GROUP - 1))
-        def _():
-            bring_in(c + GROUP)
+    @pl.loop(0, CHUNKS // GROUP)
+    def _(block):
+        for t in range(STEPS):
+
+            @pl.loop(0, GROUP)
+            def _(k, t=t):
+                c = block * GROUP + k
+                advance(c, t)
+                if t == STEPS - 1:
+
+                    @pl.when(block < CHUNKS // GROUP - 1)
+                    def _():
+                        bring_in(c + GROUP)
 
     gram = jnp.zeros((PROBES, PROBES), jnp.float32)
     for t in range(STEPS):
@@ -479,7 +484,7 @@
         q_out[:, pl.ds(128 * half, 128)] = dot_nt(block, pair)
 
     for c in range(CHUNKS):
-        whole = field.at[STEPS, c, pl.ds(WIDTH, CX)]
+        whole = field[STEPS].at[c, pl.ds(WIDTH, CX)]
         pltpu.make_async_copy(whole, whole, store_sem.at[c]).wait()
 
 
@@ -507,10 +512,11 @@
                 smem,
             ],
             out_specs=(pl.BlockSpec(memory_space=pl.ANY), vmem, vmem),
-            scratch_shapes=[
-                pltpu.VMEM((STEPS + 1, CHUNKS, CX + 2 * WIDTH, CY, CHUNK, CZ), f32),
+            scratch_shapes=[pltpu.VMEM((CHUNKS, CX + 2 * WIDTH, CY, CHUNK, CZ), f32)] * (STEPS + 1)
+            + [
                 pltpu.VMEM((CHUNKS, CX * CY * CHUNK, 2 * CZ), jnp.bfloat16),
                 pltpu.VMEM((2 * CZ, 2 * CZ), jnp.bfloat16),
+                pltpu.VMEM((CX * CY * CHUNK, CZ), f32),
                 pltpu.SMEM((recs,), jnp.int32),
                 pltpu.SMEM((recs,), jnp.int32),
                 pltpu.VMEM((CX * CY, CHUNK, CZ), f32),

time: 142 us -> 89.7 us (0.63)
  Pallas kernels: 135 us -> 82.8 us
    pallas_call x1, Pallas kernels: 135 us -> 82.8 us  [per_device(): pl.pallas_call(functools.partial(kernel, n_grp, n_slab), out_shape=(jax.S...]
where the time goes in v3:
time: 89.7 us; the launch traced here: 89.5 us
  Pallas kernels  82.8 us (92%)
  local copies, waits for them, and re-layouts  6.06 us (7%)
    pallas_call x1, Pallas kernels, per_device(): pl.pallas_call(functools.partial(kernel, n_grp, n_slab), out_shape=(jax.S...  82.8 us
    unnamed x7, local copies, waits for them, and re-layouts  6.06 us

profile of v3, /device:TPU:1, one launch (start us, length us, event | category | flops | bytes accessed | tf_op | source)
XLA Modules:
  0.0 89.5 jit_solution(6053486404689074886)
XLA Ops:
  0.6 82.8 %shard_map.76 = (f32[64,16,8,128]{3,2,1,0:T(8,128)}, f32[256,256]{1,0:T(8,128)}, f32[64,64]{1,0:T(8,128)}) custom-call(f32[64,16,8,128]{3,2,1,0:T(8,128)} %probes.1, f32[16,8,128]{2,1,0:T(8,128)} %courant.1, s32[64]{0:T(128)} %cell.1, s32[64]{0:T(128)} %bitcast.1, f32[64]{0:T(128)} %weight.1), custom_call_target="tpu_custom_call" | custom-call | tf_op jit(solution)/shard_map/pallas_call | solution.py:500
  83.4 0.0 copy-start
  83.4 0.0 copy-start.1
  83.4 4.7 %copy.11 = f32[64,16,8,128]{3,2,1,0:T(8,128)} copy(f32[64,16,8,128]{3,2,1,0:T(8,128)} %get-tuple-element.6) | data formatting | bytes 8388608
  88.2 0.0 copy-done
  88.2 0.7 copy.12
  88.9 0.0 copy-done.1
  88.9 0.6 copy.13
Async XLA Ops:
  83.4 4.8 %copy-start = (f32[256,256]{1,0:T(8,128)S(1)}, f32[256,256]{1,0:T(8,128)}, u32[]{:S(2)}) copy-start(f32[256,256]{1,0:T(8,128)} %get-tuple-element.7) | copy-start | bytes 786436
  83.4 5.5 %copy-start.1 = (f32[64,64]{1,0:T(8,128)S(1)}, f32[64,64]{1,0:T(8,128)}, u32[]{:S(2)}) copy-start(f32[64,64]{1,0:T(8,128)} %get-tuple-element.8) | copy-start | bytes 49156

commit v4 on v3

--- a/solution.py
+++ b/solution.py
@@ -62,8 +62,8 @@
     owner,
     weight,
     wave_out,
-    q_out,
-    r_out,
+    incoming,
+    gram_out,
     field_0,
     field_1,
     field_2,
@@ -82,7 +82,7 @@
     z_map,
     traces,
     outgoing,
-    incoming,
+    shares,
     sum_a,
     sum_b,
     sum_c,
@@ -124,10 +124,21 @@
             barrier, inc=1, device_id={"slab": lax.rem(s + k, n_slab)}, device_id_type=MESH
         )
 
-    @pl.loop(1, n_grp)
+    n_y = 8
+    n_x = n_slab // n_y
+    place_y = s % n_y
+    place_x = s // n_y
+
+    @pl.loop(n_x, n_x * n_grp)
     def _(k):
         pl.semaphore_signal(
-            barrier, inc=1, device_id={"grp": lax.rem(g + k, n_grp)}, device_id_type=MESH
+            barrier,
+            inc=1,
+            device_id={
+                "slab": lax.rem(place_x + k % n_x, n_x) * n_y + place_y,
+                "grp": lax.rem(g + k // n_x, n_grp),
+            },
+            device_id_type=MESH,
         )
 
     lane = lax.broadcasted_iota(jnp.int32, (8, 128), 1)
@@ -182,7 +193,7 @@
             src_ref=field[t].at[c, pl.ds(WIDTH + (1 - way) * (CX - WIDTH), WIDTH)],
             dst_ref=field[t].at[c, pl.ds(way * (CX + WIDTH), WIDTH)],
             send_sem=x_send.at[way, c],
-            recv_sem=x_recv.at[way, t, c],
+            recv_sem=x_recv.at[way, t % 2, c],
             device_id={"slab": s + 1 - 2 * way},
             device_id_type=MESH,
         )
@@ -192,7 +203,7 @@
             src_ref=z_own.at[t, c, pl.ds(1, 8)],
             dst_ref=z_halo.at[way, t, c],
             send_sem=z_send.at[way, c],
-            recv_sem=z_recv.at[way, t, c],
+            recv_sem=z_recv.at[way, t % 2, c],
             device_id={"grp": g + 1 - 2 * way},
             device_id_type=MESH,
         )
@@ -203,7 +214,7 @@
     def receiving(axis, way):
         return has[axis][way]
 
-    pl.semaphore_wait(barrier, n_slab - 1 + n_grp - 1)
+    pl.semaphore_wait(barrier, n_slab - 1 + n_x * (n_grp - 1))
 
     def pack(values):
         packed = jnp.zeros((8, 128), jnp.float32)
@@ -365,46 +376,40 @@
     gram = jnp.zeros((PROBES, PROBES), jnp.float32)
     for t in range(STEPS):
         gram = gram + dot_nt(traces[t], traces[t])
-    folded = jnp.concatenate([gram[:32], gram[32:]], axis=1)
-
-    n_y = 8
-    place_y = s % n_y
-    place_x = s // n_y
-
-    def stage_copies(buffer, count, me, base, device):
-        def one(k):
-            return pltpu.make_async_remote_copy(
-                src_ref=buffer.at[me],
-                dst_ref=buffer.at[me],
-                send_sem=sum_send.at[base + k],
-                recv_sem=sum_recv.at[base + k],
-                device_id=device(lax.rem(me + k, count)),
-                device_id_type=MESH,
-            )
-
-        return [one(k) for k in range(1, count)]
-
-    def begin(buffer, count, me, base, device, value):
-        buffer[me] = value
-        copies = stage_copies(buffer, count, me, base, device)
-        for copy in copies:
-            copy.start()
-        return copies
-
-    def finish(buffer, count, copies):
-        for copy in copies:
-            copy.wait_recv()
+    shares[...] = jnp.concatenate([gram, gram], axis=1).reshape(8, 8, 128)
+
+    def push(k, count, me, source, target, stage, device):
+        other = lax.rem(me + k, count)
+        return pltpu.make_async_remote_copy(
+            src_ref=source(other),
+            dst_ref=target.at[me],
+            send_sem=sum_send.at[stage],
+            recv_sem=sum_recv.at[stage],
+            device_id=device(other),
+            device_id_type=MESH,
+        )
+
+    def arrived(buffer, count, sem):
+        whole = buffer.at[pl.ds(0, count)]
+        return pltpu.make_async_copy(whole, whole, sem)
+
+    def added(buffer, count):
         total = buffer[0]
         for k in range(1, count):
             total = total + buffer[k]
-        for copy in copies:
-            copy.wait_send()
         return total
 
-    n_x = n_slab // n_y
-    copies = begin(
-        sum_a, n_y, place_y, 0, lambda other: {"slab": place_x * n_y + other}, folded
-    )
+    def in_row(other):
+        return {"slab": place_x * n_y + other}
+
+    def in_plane(other):
+        return {"slab": other // n_grp * n_y + place_y, "grp": other % n_grp}
+
+    sum_a[place_y] = shares[place_y]
+
+    @pl.loop(1, n_y)
+    def _(k):
+        push(k, n_y, place_y, lambda other: shares.at[other], sum_a, 0, in_row).start()
 
     own_row = jnp.zeros((1, 128), jnp.int32)
     for r in range(recs):
@@ -425,8 +430,8 @@
         return pltpu.make_async_remote_copy(
             src_ref=outgoing.at[other],
             dst_ref=incoming.at[s],
-            send_sem=a2a_send.at[k],
-            recv_sem=a2a_recv.at[k],
+            send_sem=a2a_send,
+            recv_sem=a2a_recv,
             device_id={"slab": other},
             device_id_type=MESH,
         )
@@ -438,27 +443,63 @@
     def _(k):
         to_owner(k).start()
 
-    total = finish(sum_a, n_y, copies)
-    copies = begin(
-        sum_b, n_x, place_x, n_y, lambda other: {"slab": other * n_y + place_y}, total
-    )
-    total = finish(sum_b, n_x, copies)
-    copies = begin(sum_c, n_grp, g, n_y + n_x, lambda other: {"grp": other}, total)
-    total = finish(sum_c, n_grp, copies)
-
-    low = lax.broadcasted_iota(jnp.int32, (32, 128), 1) < PROBES
+    plane = n_x * n_grp
+    place = place_x * n_grp + g
+    arrived(sum_a, n_y - 1, sum_recv.at[0]).wait()
+    sum_b[place] = added(sum_a, n_y)
+
+    @pl.loop(1, plane)
+    def _(k):
+        push(k, plane, place, lambda other: sum_b.at[place], sum_b, 1, in_plane).start()
+
+    arrived(sum_b, plane - 1, sum_recv.at[1]).wait()
+    sum_c[place_y] = added(sum_b, plane)
+
+    @pl.loop(1, n_y)
+    def _(k):
+        push(k, n_y, place_y, lambda other: sum_c.at[place_y], sum_c, 2, in_row).start()
+
+    arrived(sum_c, n_y - 1, sum_recv.at[2]).wait()
+    gram_out[...] = sum_c[...].reshape(PROBES, 128)
+
+    arrived(shares, n_y - 1, sum_send.at[0]).wait()
+    arrived(sum_b, plane - 1, sum_send.at[1]).wait()
+    arrived(sum_c, n_y - 1, sum_send.at[2]).wait()
+    to_self.wait()
+    arrived(outgoing, n_slab - 1, a2a_send).wait()
+    arrived(incoming, n_slab - 1, a2a_recv).wait()
+
+    for c in range(CHUNKS):
+        whole = field[STEPS].at[c, pl.ds(WIDTH, CX)]
+        pltpu.make_async_copy(whole, whole, store_sem.at[c]).wait()
+
+
+def finishing(count, wave_in, incoming, total, wave_out, q_out, r_out, held, sem):
+    def chunk(ref, c):
+        return ref.at[pl.ds(c * CHUNK, CHUNK)]
+
+    into = [
+        pltpu.make_async_copy(chunk(wave_in, c), held.at[c], sem.at[0, c]) for c in range(CHUNKS)
+    ]
+    back = [
+        pltpu.make_async_copy(held.at[c], chunk(wave_out, c), sem.at[1, c]) for c in range(CHUNKS)
+    ]
+    for copy in into:
+        copy.start()
     unit = lax.broadcasted_iota(jnp.int32, (PROBES, 128), 0)
     unit_lane = lax.broadcasted_iota(jnp.int32, (PROBES, 128), 1)
-    left = jnp.concatenate([total, pltpu.roll(total, PROBES, 1)], axis=0)
     work = jnp.where(
-        unit_lane < PROBES, left, jnp.where(unit_lane - PROBES == unit, 1.0, 0.0)
+        unit_lane < PROBES, total[...], jnp.where(unit_lane - PROBES == unit, 1.0, 0.0)
     )
     parts = [work[8 * b : 8 * b + 8] for b in range(8)]
     sub = lax.broadcasted_iota(jnp.int32, (8, 128), 0)
     for k in range(PROBES):
         b0 = k // 8
+        if k % 4 == 0 and 16 <= k < 16 + 4 * CHUNKS:
+            into[k // 4 - 4].wait()
+            back[k // 4 - 4].start()
         pivot_row = parts[b0][k % 8 : k % 8 + 1, :]
-        scaled = pivot_row / pivot_row[:, k : k + 1]
+        scaled = pivot_row * (1.0 / pivot_row[:, k : k + 1])
         for b in range(b0, 8):
             factor = parts[b][:, k : k + 1]
             if b == b0:
@@ -467,25 +508,15 @@
     work = jnp.concatenate(parts, axis=0)
     diag = jnp.sum(jnp.where(unit == unit_lane, work, 0.0), axis=1, keepdims=True)
     work = work * (1.0 / jnp.sqrt(diag))
-    rows = n_slab * n_grp * recs * STEPS
     upper = jnp.where((unit_lane >= unit) & (unit_lane < PROBES), work, 0.0)
-    r_out[...] = upper[:, :PROBES] * (1.0 / math.sqrt(rows))
-    inverse = jnp.where(unit_lane >= PROBES, work, 0.0) * math.sqrt(rows)
+    r_out[...] = upper[:, :PROBES] * (1.0 / math.sqrt(count))
+    inverse = jnp.where(unit_lane >= PROBES, work, 0.0) * math.sqrt(count)
     pair = jnp.concatenate([pltpu.roll(inverse, PROBES, 1), inverse], axis=0)
-
-    to_self.wait()
-
-    @pl.loop(1, n_slab)
-    def _(k):
-        to_owner(k).wait()
-
     for half in range(2):
-        block = incoming[:, :, pl.ds(128 * half, 128)].reshape(n_slab * CAP, 128)
-        q_out[:, pl.ds(128 * half, 128)] = dot_nt(block, pair)
-
-    for c in range(CHUNKS):
-        whole = field[STEPS].at[c, pl.ds(WIDTH, CX)]
-        pltpu.make_async_copy(whole, whole, store_sem.at[c]).wait()
+        spot = pl.ds(128 * half, 128)
+        q_out[:, spot] = dot_nt(incoming[:, spot], pair)
+    for copy in back:
+        copy.wait()
 
 
 def solution(mesh):
@@ -497,12 +528,12 @@
         f32 = jnp.float32
         smem = pl.BlockSpec(memory_space=pltpu.SMEM)
         vmem = pl.BlockSpec(memory_space=pltpu.VMEM)
-        wave, q_basis, r_factor = pl.pallas_call(
+        wave, incoming, total = pl.pallas_call(
             functools.partial(kernel, n_grp, n_slab),
             out_shape=(
                 jax.ShapeDtypeStruct((PROBES, CX, CY, CZ), f32),
-                jax.ShapeDtypeStruct((n_slab * CAP, STEPS * PROBES), f32),
-                jax.ShapeDtypeStruct((PROBES, PROBES), f32),
+                jax.ShapeDtypeStruct((n_slab, CAP, STEPS * PROBES), f32),
+                jax.ShapeDtypeStruct((PROBES, 128), f32),
             ),
             in_specs=[
                 pl.BlockSpec(memory_space=pl.ANY),
@@ -527,21 +558,21 @@
                 pltpu.VMEM((256, 256), jnp.bfloat16),
                 pltpu.VMEM((STEPS, PROBES, 128), f32),
                 pltpu.VMEM((n_slab, CAP, STEPS * PROBES), f32),
-                pltpu.VMEM((n_slab, CAP, STEPS * PROBES), f32),
-                pltpu.VMEM((8, 32, 128), f32),
-                pltpu.VMEM((n_slab // 8, 32, 128), f32),
-                pltpu.VMEM((n_grp, 32, 128), f32),
+                pltpu.VMEM((8, 8, 128), f32),
+                pltpu.VMEM((8, 8, 128), f32),
+                pltpu.VMEM((n_slab // 8 * n_grp, 8, 128), f32),
+                pltpu.VMEM((8, 8, 128), f32),
                 pltpu.SemaphoreType.DMA((CHUNKS,)),
                 pltpu.SemaphoreType.DMA((CHUNKS,)),
                 pltpu.SemaphoreType.DMA((2, CHUNKS)),
-                pltpu.SemaphoreType.DMA((2, STEPS, CHUNKS)),
+                pltpu.SemaphoreType.DMA((2, 2, CHUNKS)),
                 pltpu.SemaphoreType.DMA((2, CHUNKS)),
-                pltpu.SemaphoreType.DMA((2, STEPS, CHUNKS)),
-                pltpu.SemaphoreType.DMA((n_slab,)),
-                pltpu.SemaphoreType.DMA((n_slab,)),
+                pltpu.SemaphoreType.DMA((2, 2, CHUNKS)),
                 pltpu.SemaphoreType.DMA,
-                pltpu.SemaphoreType.DMA((8 + n_slab // 8 + n_grp,)),
-                pltpu.SemaphoreType.DMA((8 + n_slab // 8 + n_grp,)),
+                pltpu.SemaphoreType.DMA,
+                pltpu.SemaphoreType.DMA,
+                pltpu.SemaphoreType.DMA((3,)),
+                pltpu.SemaphoreType.DMA((3,)),
             ],
             compiler_params=pltpu.CompilerParams(
                 collective_id=0, has_side_effects=True, vmem_limit_bytes=56 * 1024 * 1024
@@ -553,7 +584,22 @@
             rec_owner.reshape(recs),
             trace_weight,
         )
-        return (wave, q_basis, r_factor)
+        anywhere = pl.BlockSpec(memory_space=pl.ANY)
+        return pl.pallas_call(
+            functools.partial(finishing, n_slab * n_grp * recs * STEPS),
+            out_shape=(
+                jax.ShapeDtypeStruct((PROBES, CX, CY, CZ), f32),
+                jax.ShapeDtypeStruct((n_slab * CAP, STEPS * PROBES), f32),
+                jax.ShapeDtypeStruct((PROBES, PROBES), f32),
+            ),
+            in_specs=[anywhere, vmem, vmem],
+            out_specs=(anywhere, vmem, vmem),
+            scratch_shapes=[
+                pltpu.VMEM((CHUNKS, CHUNK, CX, CY, CZ), f32),
+                pltpu.SemaphoreType.DMA((2, CHUNKS)),
+            ],
+            compiler_params=pltpu.CompilerParams(vmem_limit_bytes=62 * 1024 * 1024),
+        )(wave, incoming.reshape(n_slab * CAP, STEPS * PROBES), total)
 
     return jax.shard_map(
         per_device,

time: 89.7 us -> 84.5 us (0.942)
  local copies, waits for them, and re-layouts: 6.06 us -> 0 us
  Pallas kernels: 82.8 us -> 83.7 us
    pallas_call x0 -> x1, Pallas kernels: none -> 7.37 us  [per_device(): pl.pallas_call(functools.partial(finishing, n_slab * n_grp * recs * STEPS...]
    pallas_call x1, Pallas kernels: 82.8 us -> 76.3 us  [per_device(): pl.pallas_call(functools.partial(kernel, n_grp, n_slab), out_shape=(jax.S...]
    unnamed x7 -> x0, local copies, waits for them, and re-layouts: 6.06 us -> none
where the time goes in v4:
time: 84.5 us; the launch traced here: 84.3 us
  Pallas kernels  83.7 us (99%)
    pallas_call x1, Pallas kernels, per_device(): pl.pallas_call(functools.partial(kernel, n_grp, n_slab), out_shape=(jax.S...  76.3 us
    pallas_call x1, Pallas kernels, per_device(): pl.pallas_call(functools.partial(finishing, n_slab * n_grp * recs * STEPS...  7.37 us

profile of v4, /device:TPU:1, one launch (start us, length us, event | category | flops | bytes accessed | tf_op | source)
XLA Modules:
  0.0 84.3 jit_solution(5282465075045208904)
XLA Ops:
  0.6 76.3 %shard_map.76 = (f32[64,16,8,128]{3,2,1,0:T(8,128)}, f32[32,8,256]{2,1,0:T(8,128)}, f32[64,128]{1,0:T(8,128)}) custom-call(f32[64,16,8,128]{3,2,1,0:T(8,128)} %probes.1, f32[16,8,128]{2,1,0:T(8,128)} %courant.1, s32[64]{0:T(128)} %cell.1, s32[64]{0:T(128)} %bitcast.3, f32[64]{0:T(128)} %weight.1), custom_call_target="tpu_custom_call" | custom-call | tf_op jit(solution)/shard_map/pallas_call | solution.py:531
  77.0 7.4 %shard_map.77 = (f32[64,16,8,128]{3,2,1,0:T(8,128)}, f32[256,256]{1,0:T(8,128)}, f32[64,64]{1,0:T(8,128)}) custom-call(f32[64,16,8,128]{3,2,1,0:T(8,128)} %get-tuple-element.6.wave_in, f32[256,256]{1,0:T(8,128)} %bitcast.2, f32[64,128]{1,0:T(8,128)} %get-tuple-element.8.total), custom_call_target="tpu_custom_call" | custom-call | tf_op jit(solution)/shard_map/pallas_call | solution.py:588

commit v5 on v4

--- a/solution.py
+++ b/solution.py
@@ -17,7 +17,7 @@
 STEPS = 4
 CHUNK = 8
 CHUNKS = PROBES // CHUNK
-GROUP = 4
+PAIR = 2
 WIDTH = 4
 CAP = 8
 MESH = pl.DeviceIdType.MESH
@@ -251,7 +251,7 @@
             def _(way=way):
                 z_copy(0, c, way).start()
 
-    @pl.loop(0, GROUP)
+    @pl.loop(0, CHUNKS)
     def _(c):
         bring_in(c)
 
@@ -264,38 +264,41 @@
             field[STEPS].at[c, pl.ds(WIDTH, CX), :, p], wave_out.at[c * CHUNK + p], store_sem.at[c]
         )
 
-    def advance(c, t):
-        for way in range(2):
-
-            @pl.when(receiving(0, way))
-            def _(way=way):
-                x_copy(t, c, way).wait_recv()
-
-            @pl.when(receiving(1, way))
-            def _(way=way):
-                z_copy(t, c, way).wait_recv()
-
-        left = z_halo[0, t, c].reshape(64, 128)
-        right = z_halo[1, t, c].reshape(64, 128)
-        half = lax.broadcasted_iota(jnp.int32, (64, 128), 1) % 8 < WIDTH
+    def advance(m, t):
+        chunks = [PAIR * m + q for q in range(PAIR)]
+        for c in chunks:
+            for way in range(2):
+
+                @pl.when(receiving(1, way))
+                def _(c=c, way=way):
+                    z_copy(t, c, way).wait_recv()
+
+        here = pl.ds(PAIR * m, PAIR)
+        left = z_halo[0, t, here].reshape(PAIR * 64, 128)
+        right = z_halo[1, t, here].reshape(PAIR * 64, 128)
+        half = lax.broadcasted_iota(jnp.int32, (PAIR * 64, 128), 1) % 8 < WIDTH
         high, low = split(jnp.where(half, left, right))
         both = jnp.dot(
             jnp.concatenate([high, low], axis=1), z_map[...], preferred_element_type=jnp.float32
         )
-        z_fix[...] = (both[:, :128] + both[:, 128:]).reshape(8, 8, 128)
+        z_fix[...] = (both[:, :128] + both[:, 128:]).reshape(PAIR * 8, 8, 128)
         before = max(t - 1, 0)
-        both = jnp.dot(parts_of[c], z_band[...], preferred_element_type=jnp.float32)
+        rows = parts_of[here].reshape(PAIR * CX * CY * CHUNK, 2 * CZ)
+        both = jnp.dot(rows, z_band[...], preferred_element_type=jnp.float32)
         z_lap[...] = both[:, :128] + both[:, 128:]
 
-        @pl.loop(0, CX // 2)
-        def _(j):
-            fix = z_fix[j]
-            earlier = pl.multiple_of(16 * jnp.maximum(j - 1, 0), 16)
+        def one_chunk(q, n):
+            c = PAIR * m + q
+            j = n - q * 8
+            fix = z_fix[n]
+            earlier = jnp.maximum(n - 1, 0)
 
             if t < STEPS - 1:
-                z_own[t + 1, c, j] = pack([latest[earlier + i] for i in range(16)])
-
-            along_z = z_lap[pl.ds(pl.multiple_of(128 * j, 128), 128), :]
+                z_own[t + 1, PAIR * m + earlier // 8, n - earlier // 8 * 8] = pack(
+                    [latest[earlier * 16 + i] for i in range(16)]
+                )
+
+            along_z = z_lap[pl.ds(pl.multiple_of(128 * n, 128), 128), :]
             values = []
             for i in range(16):
                 y = i % 8
@@ -318,60 +321,60 @@
                 old = field[before][c, WIDTH + x, y]
                 value = (2.0 * center - old) + speed[x, y] * total
                 field[t + 1][c, WIDTH + x, y] = value
-                latest[16 * j + i] = value
+                latest[16 * n + i] = value
                 values.append(value)
 
             if t < STEPS - 1:
                 keep_parts(c, j, values)
 
+        for q, c in enumerate(chunks):
+            for way in range(2):
+
+                @pl.when(receiving(0, way))
+                def _(c=c, way=way):
+                    x_copy(t, c, way).wait_recv()
+
+            pl.loop(8 * q, 8 * q + 8)(functools.partial(one_chunk, q))
+            for way in range(2):
+
+                @pl.when(sending(0, way))
+                def _(c=c, way=way):
+                    x_copy(t, c, way).wait_send()
+                    if t < STEPS - 1:
+                        x_copy(t + 1, c, way).start()
+
         if t < STEPS - 1:
-            z_own[t + 1, c, 8] = pack([latest[112 + i] for i in range(16)])
+            z_own[t + 1, PAIR * m + PAIR - 1, 8] = pack(
+                [latest[PAIR * 128 - 16 + i] for i in range(16)]
+            )
+        for c in chunks:
             for way in range(2):
 
-                @pl.when(sending(0, way))
-                def _(way=way):
-                    x_copy(t, c, way).wait_send()
-                    x_copy(t + 1, c, way).start()
-
                 @pl.when(sending(1, way))
-                def _(way=way):
+                def _(c=c, way=way):
                     z_copy(t, c, way).wait_send()
-                    z_copy(t + 1, c, way).start()
+                    if t < STEPS - 1:
+                        z_copy(t + 1, c, way).start()
+
+        found = [jnp.zeros((8, 128), jnp.float32) for _ in chunks]
+        for r in range(recs):
+            row, turn = row_of[r], turn_of[r]
+            for q in range(PAIR):
+                value = pltpu.roll(latest[q * CX * CY + row], turn, 1)
+                found[q] = jnp.where(lane == r, value, found[q])
+        for c, value in zip(chunks, found):
+            traces[t, pl.ds(c * CHUNK, CHUNK), :] = value * weights
 
         if t == STEPS - 1:
-            for way in range(2):
-
-                @pl.when(sending(0, way))
-                def _(way=way):
-                    x_copy(t, c, way).wait_send()
-
-                @pl.when(sending(1, way))
-                def _(way=way):
-                    z_copy(t, c, way).wait_send()
-
-        found = jnp.zeros((8, 128), jnp.float32)
-        for r in range(recs):
-            value = pltpu.roll(latest[row_of[r]], turn_of[r], 1)
-            found = jnp.where(lane == r, value, found)
-        traces[t, pl.ds(c * CHUNK, CHUNK), :] = found * weights
-
-        if t == STEPS - 1:
-            for p in range(CHUNK):
-                store(c, p).start()
-
-    @pl.loop(0, CHUNKS // GROUP)
-    def _(block):
-        for t in range(STEPS):
-
-            @pl.loop(0, GROUP)
-            def _(k, t=t):
-                c = block * GROUP + k
-                advance(c, t)
-                if t == STEPS - 1:
-
-                    @pl.when(block < CHUNKS // GROUP - 1)
-                    def _():
-                        bring_in(c + GROUP)
+            for c in chunks:
+                for p in range(CHUNK):
+                    store(c, p).start()
+
+    for t in range(STEPS):
+
+        @pl.loop(0, CHUNKS // PAIR)
+        def _(m, t=t):
+            advance(m, t)
 
     gram = jnp.zeros((PROBES, PROBES), jnp.float32)
     for t in range(STEPS):
@@ -547,14 +550,14 @@
             + [
                 pltpu.VMEM((CHUNKS, CX * CY * CHUNK, 2 * CZ), jnp.bfloat16),
                 pltpu.VMEM((2 * CZ, 2 * CZ), jnp.bfloat16),
-                pltpu.VMEM((CX * CY * CHUNK, CZ), f32),
+                pltpu.VMEM((PAIR * CX * CY * CHUNK, CZ), f32),
                 pltpu.SMEM((recs,), jnp.int32),
                 pltpu.SMEM((recs,), jnp.int32),
-                pltpu.VMEM((CX * CY, CHUNK, CZ), f32),
+                pltpu.VMEM((PAIR * CX * CY, CHUNK, CZ), f32),
                 pltpu.VMEM((CX, CY, 8, CZ), f32),
                 pltpu.VMEM((STEPS, CHUNKS, 9, 8, 128), f32),
                 pltpu.VMEM((2, STEPS, CHUNKS, 8, 8, 128), f32),
-                pltpu.VMEM((8, 8, 128), f32),
+                pltpu.VMEM((PAIR * 8, 8, 128), f32),
                 pltpu.VMEM((256, 256), jnp.bfloat16),
                 pltpu.VMEM((STEPS, PROBES, 128), f32),
                 pltpu.VMEM((n_slab, CAP, STEPS * PROBES), f32),

time: 84.5 us -> 80.9 us (0.957)
  Pallas kernels: 83.7 us -> 80.1 us
    pallas_call x1, Pallas kernels: 76.3 us -> 72.8 us  [per_device(): pl.pallas_call(functools.partial(kernel, n_grp, n_slab), out_shape=(jax.S...]
where the time goes in v5:
time: 80.9 us; the launch traced here: 80.8 us
  Pallas kernels  80.1 us (99%)
    pallas_call x1, Pallas kernels, per_device(): pl.pallas_call(functools.partial(kernel, n_grp, n_slab), out_shape=(jax.S...  72.8 us
    pallas_call x1, Pallas kernels, per_device(): pl.pallas_call(functools.partial(finishing, n_slab * n_grp * recs * STEPS...  7.38 us

profile of v5, /device:TPU:1, one launch (start us, length us, event | category | flops | bytes accessed | tf_op | source)
XLA Modules:
  0.0 80.8 jit_solution(10658027710721545427)
XLA Ops:
  0.6 72.8 %shard_map.76 = (f32[64,16,8,128]{3,2,1,0:T(8,128)}, f32[32,8,256]{2,1,0:T(8,128)}, f32[64,128]{1,0:T(8,128)}) custom-call(f32[64,16,8,128]{3,2,1,0:T(8,128)} %probes.1, f32[16,8,128]{2,1,0:T(8,128)} %courant.1, s32[64]{0:T(128)} %cell.1, s32[64]{0:T(128)} %bitcast.3, f32[64]{0:T(128)} %weight.1), custom_call_target="tpu_custom_call" | custom-call | tf_op jit(solution)/shard_map/pallas_call | solution.py:534
  73.4 7.4 %shard_map.77 = (f32[64,16,8,128]{3,2,1,0:T(8,128)}, f32[256,256]{1,0:T(8,128)}, f32[64,64]{1,0:T(8,128)}) custom-call(f32[64,16,8,128]{3,2,1,0:T(8,128)} %get-tuple-element.6.wave_in, f32[256,256]{1,0:T(8,128)} %bitcast.2, f32[64,128]{1,0:T(8,128)} %get-tuple-element.8.total), custom_call_target="tpu_custom_call" | custom-call | tf_op jit(solution)/shard_map/pallas_call | solution.py:591
